TPU v7x, 128 devices: a whole 4x4x4 slice. The times are simulated.
128 devices in a mesh: row: 8 (over x, core), col: 16 (over y, z).
Axes of the slice: x: 4, y: 4, z: 4, core: 2. Of those that a mesh axis runs over, the one named last changes fastest.
Arguments:
- features: bfloat16 [65536, 1024], P(('row', 'col')), may hold values from -6 to 6
- neighbours: int32 [65536, 16], P(('row', 'col')), may hold values from 0 to 3583, as said below
- degrees: int32 [65536], P(('row', 'col')), may hold values from 1 to 16, as said below
- send_rows: int32 [128, 2048], P(('row', 'col')), may hold values from 0 to 511
- send_count: int32 [128, 128], P(('row', 'col')), may hold values from 8 to 16, as said below
- hub_rows: int32 [1024], P(('row', 'col')), may hold values from 0 to 511, as said below
- w_self: bfloat16 [1024, 1024], replicated, may hold values from -0.1875 to 0.1875
- w_neigh: bfloat16 [1024, 1024], replicated, may hold values from -0.1875 to 0.1875
- bias_term: float32 [1024], replicated, may hold values from -3 to 3
- cotangent: bfloat16 [65536, 1024], P(('row', 'col')), may hold values from -6 to 6
Outputs:
- hidden: bfloat16 [65536, 1024], P(('row', 'col'))
- grad_x: bfloat16 [65536, 1024], P(('row', 'col'))
- grad_self: bfloat16 [1024, 1024], replicated
- grad_neigh: bfloat16 [1024, 1024], replicated
Inputs may be any that keep to these rules, and one draw needn't show every extreme that they name: neighbours of partition d point to its own rows (below 512), to live slots of arrived_d only (row 512 + p * 16 + s with p != d and s < send_count[p, d]), or to hub rows; entries at j >= degrees[i] also lie in the table. `degrees`: every seed has at least one neighbour. `send_count`: each partition sends between 8 and 16 live rows to each partition, and exactly 16 to the next one. `hub_rows`: the 8 hub rows of a partition are distinct.
All inputs are finite; a program needn't handle non-finite values.
Results may differ from a plain program's by a relative error of at most 0.0064.
Values may be sent and summed in bfloat16 or wider, within the bound.
A program may use at most 128 MiB of HBM per device.

v0:
```python
import jax
import jax.numpy as jnp
from jax import lax
from jax.sharding import PartitionSpec as P


def silu_slope(pre_act):
    sigmoid_val = jax.nn.sigmoid(pre_act)
    return sigmoid_val * (1.0 + pre_act * (1.0 - sigmoid_val))


def on_device(
    features,
    neighbours,
    degrees,
    send_rows,
    send_count,
    hub_rows,
    w_self,
    w_neigh,
    bias_term,
    cotangent,
):
    n_row = lax.axis_size("row")
    n_col = lax.axis_size("col")
    n_dev = n_row * n_col
    n_local, feat_width = features.shape
    fanout = neighbours.shape[1]
    capacity = send_rows.shape[1] // n_dev
    tile_size = min(512, n_local)
    n_tiles = n_local // tile_size
    slot_live = (
        jnp.arange(capacity, dtype=jnp.int32)[None, :] < send_count.reshape(n_dev, 1)
    ).reshape(-1, 1)
    outgoing = jnp.where(slot_live, features[send_rows[0]], jnp.zeros((), jnp.bfloat16))
    arrived = lax.all_to_all(outgoing, ("row", "col"), split_axis=0, concat_axis=0, tiled=True)
    own_hubs = features[hub_rows]
    all_hubs = lax.all_gather(own_hubs, ("row", "col"), axis=0, tiled=True)
    src_table = jnp.concatenate([features, arrived, all_hubs], 0)
    table_len = src_table.shape[0]
    live_mask = jnp.arange(fanout, dtype=jnp.int32)[None, :] < degrees[:, None]
    inv_deg = 1.0 / degrees.astype(jnp.float32)

    def gather_tile(tile_index):
        tile_live = live_mask.astype(jnp.bfloat16)
        picked = src_table[neighbours]
        return jnp.einsum("nf,nfd->nd", tile_live, picked, preferred_element_type=jnp.float32)

    summed = lax.map(gather_tile, jnp.arange(n_tiles, dtype=jnp.int32)).reshape(n_local, feat_width)
    aggregate = (summed * inv_deg[:, None]).astype(jnp.bfloat16)
    pre_act = (
        jnp.dot(features, w_self, preferred_element_type=jnp.float32)
        + jnp.dot(aggregate, w_neigh, preferred_element_type=jnp.float32)
        + bias_term[None, :]
    )
    hidden = jax.nn.silu(pre_act).astype(jnp.bfloat16)
    d_pre = (cotangent.astype(jnp.float32) * silu_slope(pre_act)).astype(jnp.bfloat16)
    self_part = lax.dot_general(
        features, d_pre, (((0,), (0,)), ((), ())), preferred_element_type=jnp.float32
    )
    neigh_part = lax.dot_general(
        aggregate, d_pre, (((0,), (0,)), ((), ())), preferred_element_type=jnp.float32
    )
    grad_self, grad_neigh = lax.psum((self_part, neigh_part), ("row", "col"))
    d_agg = (
        lax.dot_general(
            d_pre, w_neigh, (((1,), (1,)), ((), ())), preferred_element_type=jnp.float32
        )
        * inv_deg[:, None]
    )
    d_own = lax.dot_general(
        d_pre, w_self, (((1,), (1,)), ((), ())), preferred_element_type=jnp.float32
    )

    def spread_tile(tile_index, d_table):
        target = jnp.where(live_mask, neighbours, table_len)
        updates = jnp.broadcast_to(d_agg[:, None, :], (tile_size, fanout, feat_width))
        return d_table.at[target.reshape(-1)].add(updates.reshape(-1, feat_width), mode="drop")

    d_table = lax.fori_loop(
        0, n_tiles, spread_tile, jnp.zeros((table_len, feat_width), jnp.float32)
    )
    n_slots = n_dev * capacity
    d_local = d_table[:n_local]
    d_arrived = d_table[n_local : n_local + n_slots]
    d_hubs = d_table[n_local + n_slots :]
    returned = lax.all_to_all(
        d_arrived.astype(jnp.bfloat16), ("row", "col"), split_axis=0, concat_axis=0, tiled=True
    ).astype(d_arrived.dtype)
    hub_back = lax.psum_scatter(d_hubs, ("row", "col"), scatter_dimension=0, tiled=True)
    grad_x = d_own + d_local
    grad_x = grad_x.at[send_rows[0]].add(jnp.where(slot_live, returned, 0.0))
    grad_x = grad_x.at[hub_rows].add(hub_back)
    return (
        hidden,
        grad_x.astype(jnp.bfloat16),
        grad_self.astype(jnp.bfloat16),
        grad_neigh.astype(jnp.bfloat16),
    )


def solution(mesh):
    in_specs = (
        P(("row", "col"), None),
        P(("row", "col"), None),
        P(("row", "col")),
        P(("row", "col"), None),
        P(("row", "col"), None),
        P(("row", "col")),
        P(),
        P(),
        P(),
        P(("row", "col"), None),
    )
    out_specs = (P(("row", "col"), None), P(("row", "col"), None), P(), P())
    return jax.shard_map(
        on_device, mesh=mesh, in_specs=in_specs, out_specs=out_specs, check_vma=False
    )
```

profile of v0, /device:TPU:0, one launch (start us, length us, event | category | flops | bytes accessed | tf_op | source)
XLA Modules:
  0.0 957.6 jit_solution(10110251208233370689)
XLA Ops:
  7.2 0.0 copy-start
  7.2 0.0 all-gather.3.cloned.1.call-start
  7.2 0.8 compare_select_fusion.3
  8.0 2.5 gather_fusion.1
  10.6 0.0 all-gather.3.cloned.1.call-update
  10.6 0.7 compare_select_fusion.2
  11.3 0.0 copy-start.9
  11.3 12.3 %gather_fusion = bf16[2048,1024]{1,0:T(8,128)(2,1)} fusion(bf16[512,1024]{1,0:T(8,128)(2,1)} %param.10, s32[2048]{0:T(1024)S(1)} %broadcast_clamp_fusion.1), kind=kCustom, calls=%fused_computation | custom fusion | bytes 8396800 | tf_op jit(solution)/shard_map/gather | solution.py:35
  23.7 0.0 copy-done.9
  23.7 0.1 iota_compare_fusion
  23.8 3.8 broadcast_select_fusion
  27.6 0.0 copy-start.8
  27.6 0.0 copy-start.7
  27.6 0.0 copy-start.1
  27.6 11.7 %all-to-all-start = ((bf16[128,16,1024]{2,1,0:T(8,128)(2,1)}), bf16[128,16,1024]{2,1,0:T(8,128)(2,1)}, u32[]{:S(2)}, u32[]{:S(2)}) async-start(bf16[128,16,1024]{2,1,0:T(8,128)(2,1)} %broadcast_select_fusion), calls=%async_computation | async-start | bytes 8388608 | tf_op jit(solution)/shard_map/all_to_all | solution.py:36
  39.3 0.0 reduce-scatter.2.cloned.1.call-start
  39.3 0.0 copy-done.8
  39.4 0.4 copy.18
  39.8 0.0 copy-done.7
  39.8 0.8 copy.15
  40.7 1.1 reshape.128
  41.8 0.8 copy.16
  42.6 1.1 reshape.107
  43.7 0.0 copy-done.1
  43.7 4.2 fusion.11
  48.0 64.1 %all-gather.3.cloned.1.call-done = bf16[1024,1024]{1,0:T(8,128)(2,1)} async-done(((bf16[8,1024]{1,0:T(8,128)(2,1)}), bf16[1024,1024]{1,0:T(8,128)(2,1)}) %all-gather.3.cloned.1.call-update) | async-done | bytes 2097168 | tf_op jit(solution)/shard_map/all_gather | solution.py:38
  112.1 0.0 all-to-all-done
  112.1 6.3 pad_maximum_fusion
  118.3 44.7 %gather_fusion.2 = bf16[8192,1024]{1,0:T(8,128)(2,1)} fusion(bf16[3584,1024]{1,0:T(8,128)(2,1)} %pad_maximum_fusion, s32[8192]{0:T(1024)S(1)} %broadcast_clamp_fusion), kind=kCustom, calls=%fused_computation.2 | custom fusion | bytes 33587200 | tf_op jit(solution)/shard_map/while/body/eval_jaxpr/gather | solution.py:46
  163.0 0.0 copy-start.10
  163.0 0.0 copy-start.11
  163.0 0.0 copy-start.12
  163.0 8.6 fusion.12
  171.6 0.0 copy-done
  171.6 0.0 copy-done.10
  171.6 0.0 copy-done.11
  171.7 0.0 copy-done.12
  171.7 0.0 copy-start.2
  171.7 3.0 multiply_convert_fusion
  174.7 0.0 copy-done.2
  174.7 0.0 copy-start.4
  174.7 1.3 convolution_multiply_fusion
  176.0 0.0 copy-done.4
  176.1 11.3 %broadcast_in_dim.67 = f32[512,16,1024]{2,1,0:T(8,128)} broadcast(f32[512,1024]{1,0:T(8,128)S(1)} %convolution_multiply_fusion), dimensions={0,2} | broadcast | bytes 35651584 | tf_op jit(solution)/shard_map/while/body/eval_jaxpr/broadcast_in_dim | solution.py:77
  187.4 77.1 %scatter_custom_fusion = f32[3584,1024]{1,0:T(8,128)} fusion(s32[8192]{0:T(1024)S(1)} %bitcast.40, f32[8192,1024]{1,0:T(8,128)} %bitcast.37, f32[]{:T(128)} %constant.13.clone.1), kind=kCustom, calls=%fused_computation.10 | custom fusion | flops 8388608 | bytes 14680576 | tf_op jit(solution)/shard_map/while/body/eval_jaxpr/scatter-add | solution.py:78
  264.4 4.7 slice.21
  269.2 0.0 reduce-scatter.2.cloned.1.call-update
  269.2 6.0 slice.24
  275.2 6.6 all-to-all-start.1
  281.8 0.1 lt.79
  281.9 0.0 copy-start.5
  281.9 4.6 convolution_bitcast_fusion
  286.5 0.0 copy-done.3
  286.5 0.0 copy-done.5
  286.5 3.5 fusion.8
  290.1 147.6 %all-reduce.2 = (bf16[1024,1024]{0,1:T(8,128)(2,1)}, bf16[1024,1024]{1,0:T(8,128)(2,1)}) all-reduce(f32[1024,1024]{0,1:T(8,128)} %convolution_bitcast_fusion, f32[1024,1024]{1,0:T(8,128)} %fusion.8), channel_id=1, replica_groups=mesh['row'=8,'col'=16] {'row','col'}, use_global_device_ids=true, to_apply=%region_4.5 | all-reduce | flops 2097152 | bytes 12582912 | tf_op jit(solution)/shard_map/psum | solution.py:64
  437.7 4.0 copy.17
  441.7 0.0 copy-done.6
  441.7 4.9 slice_add_fusion
  446.6 0.0 all-to-all-done.1
  446.6 21.7 %scatter_custom_fusion.1 = f32[512,1024]{1,0:T(8,128)} fusion(f32[512,1024]{1,0:T(8,128)} %slice_add_fusion, s32[2048]{0:T(1024)S(1)} %bitcast.42, bf16[2048,1024]{1,0:T(8,128)(2,1)} %bitcast.13, f32[]{:T(128)} %constant.13.clone.1, pred[2048]{0:T(1024)(128)(4,1)S(1)} %lt.79), kind=kCustom, calls=%fused_computation.8 | custom fusion | flops 6291456 | bytes 6294016 | tf_op jit(solution)/shard_map/scatter-add | solution.py:92
  468.3 476.0 %reduce-scatter.2.cloned.1.call-done = f32[8,1024]{1,0:T(8,128)} async-done(((f32[1024,1024]{1,0:T(8,128)}), f32[8,1024]{1,0:T(8,128)}) %reduce-scatter.2.cloned.1.call-update) | async-done | bytes 32784 | tf_op jit(solution)/shard_map/reduce_scatter | solution.py:90
  944.3 3.7 scatter_fusion
  948.0 2.7 convert_element_type.40
  (9 shorter events, 0.1 us)
Async XLA Ops:
  7.2 164.5 %copy-start = (bf16[1024,1024]{1,0:T(8,128)(2,1)S(1)}, bf16[1024,1024]{1,0:T(8,128)(2,1)}, u32[]{:S(2)}) copy-start(bf16[1024,1024]{1,0:T(8,128)(2,1)} %param.17) | copy-start | bytes 6291460
  7.2 104.9 %all-gather.3.cloned.1.call-start = ((), (), s32[]{:S(2)}) async-start(), calls=%async_computation.4 | async-start | bytes 2113536 | tf_op jit(solution)/shard_map/all_gather | solution.py:38
  11.3 12.3 %copy-start.9 = (s32[1,128]{1,0:T(1,128)S(1)}, s32[1,128]{1,0:T(1,128)}, u32[]{:S(2)}) copy-start(s32[1,128]{1,0:T(1,128)} %param.14) | copy-start | bytes 1540
  27.6 11.8 %copy-start.8 = (s32[512]{0:T(512)S(1)}, s32[512]{0:T(512)}, u32[]{:S(2)}) copy-start(s32[512]{0:T(512)} %param.12) | copy-start | bytes 6148
  27.6 12.2 %copy-start.7 = (s32[512,16]{0,1:T(8,128)S(1)}, s32[512,16]{0,1:T(8,128)}, u32[]{:S(2)}) copy-start(s32[512,16]{0,1:T(8,128)} %param.11) | copy-start | bytes 98308
  27.6 16.1 %copy-start.1 = (bf16[512,1024]{1,0:T(8,128)(2,1)S(1)}, bf16[512,1024]{1,0:T(8,128)(2,1)}, u32[]{:S(2)}) copy-start(bf16[512,1024]{1,0:T(8,128)(2,1)} %param.10) | copy-start | bytes 3145732
  27.6 84.5 %all-to-all-start = ((bf16[128,16,1024]{2,1,0:T(8,128)(2,1)}), bf16[128,16,1024]{2,1,0:T(8,128)(2,1)}, u32[]{:S(2)}, u32[]{:S(2)}) async-start(bf16[128,16,1024]{2,1,0:T(8,128)(2,1)} %broadcast_select_fusion), calls=%async_computation | async-start | bytes 8388608 | tf_op jit(solution)/shard_map/all_to_all | solution.py:36
  39.3 905.0 %reduce-scatter.2.cloned.1.call-start = ((), (), s32[]{:S(2)}) async-start(), calls=%async_computation.3 | async-start | bytes 4227072 | tf_op jit(solution)/shard_map/reduce_scatter | solution.py:90
  163.0 8.7 copy-start.10
  163.0 8.7 copy-start.11
  163.0 8.7 copy-start.12
  171.7 3.1 copy-start.2
  174.7 1.3 copy-start.4
  275.2 171.4 %all-to-all-start.1 = ((bf16[128,16,1024]{2,1,0:T(8,128)(2,1)}), bf16[128,16,1024]{2,1,0:T(8,128)(2,1)}, u32[]{:S(2)}, u32[]{:S(2)}) async-start(bf16[128,16,1024]{2,1,0:T(8,128)(2,1)} %bitcast.39), calls=%async_computation.1 | async-start | bytes 8388608 | tf_op jit(solution)/shard_map/all_to_all | solution.py:87
  281.9 4.6 copy-start.3
  281.9 4.6 copy-start.5
  437.7 4.0 copy-start.6
Sparse Core Ops, SparseCore 0:
  11.5 100.4 all-gather.2
  269.3 674.8 reduce-scatter.1
where the time goes:
time: 959 us; the launch traced here: 958 us
  waiting for transfers between devices  540 us (56%)
  blocking collectives  148 us (15%)
  other arithmetic  117 us (12%)
  local copies, waits for them, and re-layouts  90.1 us (9%)
  matrix products  30.2 us (3%)
  starting transfers between devices  18.4 us (2%)
  between operations  14.3 us (1%)
    reduce_scatter x1, waiting for transfers between devices, on_device(): lax.psum_scatter(d_hubs, ('row', 'col'), scatter_dimension=0, tiled=True)  476 us
    psum x1, blocking collectives, on_device(): grad_self, grad_neigh = lax.psum((self_part, neigh_part), ('row', 'col'))  148 us
    scatter-add x1, other arithmetic, spread_tile(): d_table.at[target.reshape(-1)]  77.1 us
    all_gather x1, waiting for transfers between devices, on_device(): all_hubs = lax.all_gather(own_hubs, ('row', 'col'), axis=0, tiled=True)  64.1 us
    gather x1, local copies, waits for them, and re-layouts, gather_tile(): picked = src_table[neighbours]  44.7 us
    scatter-add x1, other arithmetic, on_device(): grad_x = grad_x.at[send_rows[0]].add(jnp.where(slot_live, returned, 0.0))  21.7 us
  transfers between devices with their start and end apart: 4, of which 2 were waited for; matrix products, arithmetic and copies ran while one was open for 7% of the time, Pallas kernels for 0%

commit v1 on v0

v1 whole, which is shorter than its diff:
```python
import functools
import jax
import jax.numpy as jnp
from jax import lax
from jax.experimental import pallas as pl
from jax.experimental.pallas import tpu as pltpu
from jax.sharding import PartitionSpec as P

MESH = pl.DeviceIdType.MESH
COLS = ((0, 384), (384, 384), (768, 256))
ORDERS = (("x", "y", "z"), ("y", "z", "x"), ("z", "x", "y"))


def where_am_i():
    row = lax.axis_index("row")
    col = lax.axis_index("col")
    return {"x": row // 2, "core": lax.rem(row, 2), "y": col // 4, "z": lax.rem(col, 4)}


def device_at(place):
    return (place["x"] * 2 + place["core"], place["y"] * 4 + place["z"])


def shifted(place, dim, step):
    other = dict(place)
    other[dim] = lax.rem(place[dim] + step, 2 if dim == "core" else 4)
    return other


def greet(place):
    barrier = pltpu.get_barrier_semaphore()
    peers = [shifted(place, "core", 1)]
    peers += [shifted(place, dim, step) for dim in "xyz" for step in (1, 2, 3)]
    for peer in peers:
        pl.semaphore_signal(barrier, inc=1, device_id=device_at(peer), device_id_type=MESH)
    pl.semaphore_wait(barrier, len(peers))


def remote(src, dst, send_sem, recv_sem, peer):
    return pltpu.make_async_remote_copy(
        src_ref=src,
        dst_ref=dst,
        send_sem=send_sem,
        recv_sem=recv_sem,
        device_id=device_at(peer),
        device_id_type=MESH,
    )


def window(ref, fixed, part, dims):
    start, size = COLS[part]
    index = tuple(fixed.get(dim, slice(None)) for dim in dims)
    return ref.at[index + (slice(None), pl.ds(start, size))]


ALL_DIMS = ("x", "core", "y", "z")


def spread_blocks(place, out, send_sem, recv_sem):
    for stage in range(3):
        copies = []
        for part, order in enumerate(ORDERS):
            dim = order[2 - stage]
            fixed = {"core": place["core"]}
            for known in order[: 3 - stage]:
                fixed[known] = place[known]
            block = window(out, fixed, part, ALL_DIMS)
            for step in (1, 2, 3):
                slot = (stage * 3 + part) * 3 + step - 1
                copy = remote(block, block, send_sem.at[slot], recv_sem.at[slot], shifted(place, dim, step))
                copy.start()
                copies.append(copy)
        for copy in copies:
            copy.wait()
    half = out.at[:, place["core"]]
    copy = remote(half, half, send_sem.at[27], recv_sem.at[27], shifted(place, "core", 1))
    copy.start()
    copy.wait()


def gather_kernel(own, out, send_sem, recv_sem):
    place = where_am_i()
    greet(place)
    out[place["x"], place["core"], place["y"], place["z"]] = own[...]
    spread_blocks(place, out, send_sem, recv_sem)


def gather_blocks(own, collective_id):
    rows, width = own.shape
    out = pl.pallas_call(
        gather_kernel,
        out_shape=jax.ShapeDtypeStruct((4, 2, 4, 4, rows, width), own.dtype),
        in_specs=[pl.BlockSpec(memory_space=pltpu.VMEM)],
        out_specs=pl.BlockSpec(memory_space=pltpu.VMEM),
        scratch_shapes=[pltpu.SemaphoreType.DMA((28,)), pltpu.SemaphoreType.DMA((28,))],
        compiler_params=pltpu.CompilerParams(collective_id=collective_id, has_side_effects=True),
        name="gather_blocks",
    )(own)
    return out.reshape(128 * rows, width)


def reduce_kernel(n, *refs):
    sources, refs = refs[:n], refs[n:]
    outs, refs = refs[:2], refs[2:]
    bufs = [refs[i * 7 : i * 7 + 7] for i in range(n)]
    send_sem, recv_sem, ag_send, ag_recv = refs[7 * n :]
    place = where_am_i()
    greet(place)
    f32 = jnp.float32
    partner = shifted(place, "core", 1)
    copies = []
    for i, src in enumerate(sources):
        copy = remote(src.at[:, partner["core"]], bufs[i][0], send_sem.at[i], recv_sem.at[i], partner)
        copy.start()
        copies.append(copy)
    for i, src in enumerate(sources):
        copies[i].wait()
        got, total = bufs[i][0], bufs[i][1]

        def add(t, _, src=src, got=got, total=total):
            x, y, z = t // 16, lax.rem(t // 4, 4), lax.rem(t, 4)
            total[x, y, z] = (src[x, place["core"], y, z].astype(f32) + got[x, y, z].astype(f32)).astype(jnp.bfloat16)
            return 0

        lax.fori_loop(0, 64, add, 0)
    for stage in range(3):
        started = []
        for part, order in enumerate(ORDERS):
            dim = order[stage]
            dims = [d for d in "xyz" if d not in order[:stage]]
            for i in range(n):
                held = bufs[i][1 + 2 * stage]
                came = bufs[i][2 + 2 * stage]
                mine = []
                for step in (1, 2, 3):
                    peer = shifted(place, dim, step)
                    slot = n + ((stage * 3 + part) * n + i) * 3 + step - 1
                    start, size = COLS[part]
                    dst = came.at[(step - 1,) + (slice(None),) * (len(dims) - 1) + (slice(None), pl.ds(start, size))]
                    copy = remote(
                        window(held, {dim: peer[dim]}, part, dims), dst, send_sem.at[slot], recv_sem.at[slot], peer
                    )
                    copy.start()
                    mine.append(copy)
                started.append((part, i, dims, dim, held, came, mine))
        for part, i, dims, dim, held, came, mine in started:
            for copy in mine:
                copy.wait()
            start, size = COLS[part]
            cols = pl.ds(start, size)
            count = 4 ** (len(dims) - 1)

            def fold(t, _, part=part, i=i, dims=dims, dim=dim, held=held, came=came, cols=cols):
                rest = [d for d in dims if d != dim]
                at = {dim: place[dim]}
                if len(rest) == 2:
                    at[rest[0]], at[rest[1]] = t // 4, lax.rem(t, 4)
                elif len(rest) == 1:
                    at[rest[0]] = t
                total = held[tuple(at[d] for d in dims) + (slice(None), cols)].astype(f32)
                for k in range(3):
                    total += came[(k,) + tuple(at[d] for d in rest) + (slice(None), cols)].astype(f32)
                if len(rest):
                    nxt = bufs[i][3 + 2 * stage]
                    nxt[tuple(at[d] for d in rest) + (slice(None), cols)] = total.astype(jnp.bfloat16)
                elif i == 0:
                    outs[0][place["x"], place["core"], place["y"], place["z"], :, cols] = total.astype(jnp.bfloat16)
                else:
                    outs[1][:, cols] = total
                return 0

            if count > 1:
                lax.fori_loop(0, count, fold, 0)
            else:
                fold(0, 0)
    spread_blocks(place, outs[0], ag_send, ag_recv)


def reduce_blocks(grads, hubs, collective_id):
    width = grads.shape[1]
    operands = [a.reshape(4, 2, 4, 4, a.shape[0] // 128, width) for a in (grads, hubs)]
    scratch = []
    for a in operands:
        rows = a.shape[4]
        for shape in (
            (4, 4, 4, rows, width),
            (4, 4, 4, rows, width),
            (3, 4, 4, rows, width),
            (4, 4, rows, width),
            (3, 4, rows, width),
            (4, rows, width),
            (3, rows, width),
        ):
            scratch.append(pltpu.VMEM(shape, jnp.bfloat16))
    n = 2
    count = n + 9 * n * 3
    out, own = pl.pallas_call(
        functools.partial(reduce_kernel, n),
        out_shape=(
            jax.ShapeDtypeStruct(operands[0].shape, jnp.bfloat16),
            jax.ShapeDtypeStruct((operands[1].shape[4], width), jnp.float32),
        ),
        in_specs=[pl.BlockSpec(memory_space=pltpu.VMEM)] * 2,
        out_specs=[pl.BlockSpec(memory_space=pltpu.VMEM)] * 2,
        scratch_shapes=scratch
        + [
            pltpu.SemaphoreType.DMA((count,)),
            pltpu.SemaphoreType.DMA((count,)),
            pltpu.SemaphoreType.DMA((28,)),
            pltpu.SemaphoreType.DMA((28,)),
        ],
        compiler_params=pltpu.CompilerParams(
            collective_id=collective_id, has_side_effects=True, vmem_limit_bytes=48 * 1024 * 1024
        ),
        name="reduce_blocks",
    )(*operands)
    return out.reshape(2048, width), own


def silu_slope(pre_act):
    sigmoid_val = jax.nn.sigmoid(pre_act)
    return sigmoid_val * (1.0 + pre_act * (1.0 - sigmoid_val))


def dot(a, b, ca, cb, kind=jnp.float32):
    return lax.dot_general(a, b, (((ca,), (cb,)), ((), ())), preferred_element_type=kind)


def on_device(
    features, neighbours, degrees, send_rows, send_count, hub_rows, w_self, w_neigh, bias_term, cotangent
):
    n_dev = 128
    n_local, feat_width = features.shape
    fanout = neighbours.shape[1]
    capacity = send_rows.shape[1] // n_dev
    n_slots = n_dev * capacity
    bf16 = jnp.bfloat16
    table_len = n_local + n_slots + hub_rows.shape[0] * n_dev
    slot_live = jnp.arange(capacity, dtype=jnp.int32)[None, :] < send_count.reshape(n_dev, 1)
    live_row = jnp.where(slot_live.reshape(-1), send_rows[0], -1)
    picks = (live_row[:, None] == jnp.arange(n_local, dtype=jnp.int32)[None, :]).astype(bf16)
    outgoing = dot(picks, features, 1, 0, bf16)
    arrived = lax.all_to_all(outgoing, ("row", "col"), split_axis=0, concat_axis=0, tiled=True)
    hub_picks = (hub_rows[:, None] == jnp.arange(n_local, dtype=jnp.int32)[None, :]).astype(bf16)
    own_hubs = dot(hub_picks, features, 1, 0, bf16)
    all_hubs = gather_blocks(own_hubs, 1)

    live = jnp.arange(fanout, dtype=jnp.int32)[None, :] < degrees[:, None]
    target = jnp.where(live, neighbours, -1)
    entry = jnp.arange(table_len, dtype=jnp.int32)[None, :]
    counts = jnp.zeros((n_local, table_len), jnp.float32)
    for j in range(fanout):
        counts += (target[:, j : j + 1] == entry).astype(jnp.float32)
    counts = counts.astype(bf16)
    own_counts = counts[:, :n_local]
    slot_counts = counts[:, n_local : n_local + n_slots]
    hub_counts = counts[:, n_local + n_slots :]
    inv_deg = 1.0 / degrees.astype(jnp.float32)

    summed = dot(own_counts, features, 1, 0) + dot(hub_counts, all_hubs, 1, 0) + dot(slot_counts, arrived, 1, 0)
    aggregate = (summed * inv_deg[:, None]).astype(bf16)
    pre_act = dot(features, w_self, 1, 0) + dot(aggregate, w_neigh, 1, 0) + bias_term[None, :]
    hidden = jax.nn.silu(pre_act).astype(bf16)
    d_pre = (cotangent.astype(jnp.float32) * silu_slope(pre_act)).astype(bf16)

    d_agg = (dot(d_pre, w_neigh, 1, 1) * inv_deg[:, None]).astype(bf16)
    d_arrived = dot(slot_counts, d_agg, 0, 0, bf16)
    returned = lax.all_to_all(d_arrived, ("row", "col"), split_axis=0, concat_axis=0, tiled=True)
    grads = jnp.concatenate([dot(features, d_pre, 0, 0, bf16), dot(aggregate, d_pre, 0, 0, bf16)], 0)
    d_hubs = dot(hub_counts, d_agg, 0, 0, bf16)
    grads, hub_back = reduce_blocks(grads, d_hubs, 2)
    grad_x = dot(d_pre, w_self, 1, 1) + dot(own_counts, d_agg, 0, 0)
    grad_x = grad_x + lax.dot_general(
        hub_picks.astype(jnp.float32),
        hub_back,
        (((0,), (0,)), ((), ())),
        precision=lax.Precision.HIGHEST,
        preferred_element_type=jnp.float32,
    )
    grad_x = grad_x + dot(picks, returned, 0, 0)
    return (hidden, grad_x.astype(bf16), grads[:feat_width], grads[feat_width:])


def solution(mesh):
    split = P(("row", "col"), None)
    in_specs = (split, split, P(("row", "col")), split, split, P(("row", "col")), P(), P(), P(), split)
    out_specs = (split, split, P(), P())
    return jax.shard_map(on_device, mesh=mesh, in_specs=in_specs, out_specs=out_specs, check_vma=False)
```

time: 959 us -> 251 us (0.26)
  waiting for transfers between devices: 540 us -> 0.01 us
  Pallas kernels: 0 us -> 157 us
  blocking collectives: 148 us -> 0 us
  other arithmetic: 117 us -> 21.7 us
  local copies, waits for them, and re-layouts: 90.1 us -> 6.53 us
  matrix products: 30.2 us -> 45.1 us
  between operations: 14.3 us -> 0.94 us
    reduce_scatter x1 -> x0, waiting for transfers between devices: 476 us -> none  [on_device(): lax.psum_scatter(d_hubs, ('row', 'col'), scatter_dimension=0, tiled=True)]
    pallas_call x0 -> x2, Pallas kernels: none -> 157 us  [the longest x1 91.8 us: reduce_blocks(): pl.pallas_call(functools.partial(reduce_kernel, n), out_shape=(jax.ShapeD...]
    psum x1 -> x0, blocking collectives: 148 us -> none  [on_device(): grad_self, grad_neigh = lax.psum((self_part, neigh_part), ('row', 'col'))]
    scatter-add x3 -> x0, other arithmetic: 102 us -> none  [the longest x1 77.1 us: spread_tile(): d_table.at[target.reshape(-1)]]
    all_gather x1 -> x0, waiting for transfers between devices: 64.1 us -> none  [on_device(): all_hubs = lax.all_gather(own_hubs, ('row', 'col'), axis=0, tiled=True)]
    gather x3 -> x0, local copies, waits for them, and re-layouts: 59.5 us -> none  [the longest x1 44.7 us: gather_tile(): picked = src_table[neighbours]]
    convert_element_type x1, other arithmetic: 2.72 us -> 17.7 us  [on_device(): counts = counts.astype(bf16)]
    dot_general x7 -> x16, matrix products: 30.2 us -> 45.1 us  [the longest x15 42.7 us: dot(): lax.dot_general(a, b, (((ca,), (cb,)), ((), ())), preferred_element_type=...]
  transfers between devices with their start and end apart: 4 -> 2, of which waited for: 2 -> 0; matrix products, arithmetic and copies ran while one was open for 7% -> 16% of each run, Pallas kernels for 0% -> 63%
where the time goes in v1:
time: 251 us; the launch traced here: 250 us
  Pallas kernels  157 us (63%)
  matrix products  45.1 us (18%)
  other arithmetic  21.7 us (9%)
  starting transfers between devices  18.4 us (7%)
  local copies, waits for them, and re-layouts  6.53 us (3%)
    pallas_call x1, Pallas kernels, reduce_blocks(): pl.pallas_call(functools.partial(reduce_kernel, n), out_shape=(jax.ShapeD...  91.8 us
    pallas_call x1, Pallas kernels, gather_blocks(): pl.pallas_call(gather_kernel, out_shape=jax.ShapeDtypeStruct((4, 2, 4, 4,...  65.3 us
    dot_general x15, matrix products, dot(): lax.dot_general(a, b, (((ca,), (cb,)), ((), ())), preferred_element_type=...  42.7 us
    convert_element_type x1, other arithmetic, on_device(): counts = counts.astype(bf16)  17.7 us
    all_to_all x1, starting transfers between devices, on_device(): lax.all_to_all(outgoing, ('row', 'col'), split_axis=0, concat_axis=0, til...  11.7 us
    all_to_all x1, starting transfers between devices, on_device(): lax.all_to_all(d_arrived, ('row', 'col'), split_axis=0, concat_axis=0, ti...  6.64 us
  transfers between devices with their start and end apart: 2, of which 0 were waited for; matrix products, arithmetic and copies ran while one was open for 16% of the time, Pallas kernels for 63%

profile of v1, /device:TPU:0, one launch (start us, length us, event | category | flops | bytes accessed | tf_op | source)
XLA Modules:
  0.0 249.7 jit_solution(11469358554991266485)
XLA Ops:
  0.6 0.0 copy-start
  0.6 0.9 iota_compare_fusion.19
  1.5 0.1 lt.43
  1.6 0.7 broadcast_select_fusion
  2.3 5.2 %fusion.1 = bf16[2048,1024]{1,0:T(8,128)(2,1)} fusion(bf16[512,1024]{1,0:T(8,128)(2,1)} %param.10, s32[2048]{0:T(1024)S(1)} %broadcast_select_fusion), kind=kOutput, calls=%fused_computation.20 | convolution fusion | flops 2148532224 | bytes 5251072 | tf_op jit(solution)/shard_map/dot_general | solution.py:226
  7.6 0.0 copy-start.5
  7.6 0.0 copy-start.15
  7.6 0.0 copy-start.14
  7.6 0.0 copy-start.13
  7.6 11.7 %all-to-all-start = ((bf16[128,16,1024]{2,1,0:T(8,128)(2,1)}), bf16[128,16,1024]{2,1,0:T(8,128)(2,1)}, u32[]{:S(2)}, u32[]{:S(2)}) async-start(bf16[128,16,1024]{2,1,0:T(8,128)(2,1)} %bitcast.53), calls=%async_computation | async-start | bytes 8388608 | tf_op jit(solution)/shard_map/all_to_all | solution.py:243
  19.3 0.0 copy-done.5
  19.3 0.0 copy-done.15
  19.3 0.9 fusion.16.own
  20.2 65.3 %gather_blocks.1 = bf16[4,2,4,4,8,1024]{5,4,3,2,1,0:T(8,128)(2,1)} custom-call(bf16[8,1024]{1,0:T(8,128)(2,1)} %fusion.16.own), custom_call_target="tpu_custom_call" | custom-call | tf_op jit(solution)/shard_map/gather_blocks/pallas_call | solution.py:90
  85.5 0.0 copy-done.14
  85.6 0.0 copy-done.13
  85.6 0.0 copy-start.7
  85.6 4.3 %fusion.21 = f32[512,1024]{1,0:T(8,128)} fusion(bf16[512,1024]{1,0:T(8,128)(2,1)S(1)} %copy-done.5, bf16[1024,1024]{1,0:T(8,128)(2,1)} %param.16), kind=kOutput, calls=%fused_computation.53 | convolution fusion | flops 1073741824 | bytes 5242880 | tf_op jit(solution)/shard_map/dot_general | solution.py:226
  89.9 17.7 %add_convert_fusion = bf16[512,3584]{1,0:T(8,128)(2,1)S(1)} fusion(s32[512]{0:T(512)S(1)} %bitcast.59, s32[512]{0:T(512)S(1)} %bitcast.60, s32[512]{0:T(512)S(1)} %bitcast.61, s32[512]{0:T(512)S(1)} %bitcast.62, s32[512]{0:T(512)S(1)} %bitcast.63, s32[512]{0:T(512)S(1)} %bitcast.64, s32[512]{0:T(512)S(1)} %bitcast.65, s32[512]{0:T(512)S(1)} %bitcast.66, ...), kind=kLoop, calls=%fused_computation | loop fusion | flops 88080384 | bytes 3702784 | tf_op jit(solution)/shard_map/convert_element_type | solution.py:254
  107.7 0.0 copy-start.2
  107.7 1.8 copy-done.2
  109.5 0.0 copy-done.7
  109.5 2.6 %fusion.10 = f32[512,1024]{1,0:T(8,128)} fusion(bf16[1024,1024]{1,0:T(8,128)(2,1)S(1)} %bitcast.55, bf16[512,3584]{1,0:T(8,128)(2,1)S(1)} %add_convert_fusion), kind=kOutput, calls=%fused_computation.37 | convolution fusion | flops 1073741824 | bytes 5242880 | tf_op jit(solution)/shard_map/dot_general | solution.py:226
  112.0 0.0 all-to-all-done
  112.0 5.3 %fusion.6 = f32[512,1024]{1,0:T(8,128)S(1)} fusion(bf16[2048,1024]{1,0:T(8,128)(2,1)} %bitcast.20, bf16[512,3584]{1,0:T(8,128)(2,1)} %copy-done.2), kind=kOutput, calls=%fused_computation.32 | convolution fusion | flops 2147483648 | bytes 8388608 | tf_op jit(solution)/shard_map/dot_general | solution.py:226
  117.3 0.0 copy-done.3
  117.3 0.0 copy-done.8
  117.4 0.0 copy-start.17
  117.4 0.0 copy-start.18
  117.4 0.0 copy-start.19
  117.4 0.8 multiply_convert_fusion.3
  118.2 0.0 copy-done
  118.2 0.4 copy-done.17
  118.6 0.0 copy-done.18
  118.6 0.7 copy-done.19
  119.3 3.0 %multiply_convert_fusion.1 = (bf16[512,1024]{1,0:T(8,128)(2,1)S(1)}, bf16[512,1024]{1,0:T(8,128)(2,1)}) fusion(bf16[512,1024]{1,0:T(8,128)(2,1)S(1)} %copy-done.17, f32[1024]{0:T(1024)S(1)} %copy-done.18, f32[512,1024]{1,0:T(8,128)S(1)} %copy-done.19, bf16[512,1024]{1,0:T(8,128)(2,1)S(1)} %multiply_convert_fusion.3, bf16[1024,1024]{1,0:T(8,128)(2,1)S(1)} %copy-done), kind=kOutput, calls=%fused_computation.23 | convolution fusion | flops 1081081856 | bytes 8392704 | tf_op jit(solution)/shard_map/dot_general | solution.py:226
  122.3 0.0 copy-done.12
  122.3 1.0 copy-done.20
  123.2 1.3 multiply_convert_fusion
  124.5 0.0 copy-start.10
  124.6 4.4 %fusion.4 = bf16[2048,1024]{1,0:T(8,128)(2,1)} fusion(bf16[512,1024]{1,0:T(8,128)(2,1)S(1)} %multiply_convert_fusion, bf16[512,3584]{1,0:T(8,128)(2,1)S(1)} %copy-done.3), kind=kOutput, calls=%fused_computation.30 | convolution fusion | flops 2147483648 | bytes 7340032 | tf_op jit(solution)/shard_map/dot_general | solution.py:226
  129.0 0.0 copy-done.10
  129.0 6.6 %all-to-all-start.1 = ((bf16[128,16,1024]{2,1,0:T(8,128)(2,1)}), bf16[128,16,1024]{2,1,0:T(8,128)(2,1)}, u32[]{:S(2)}, u32[]{:S(2)}) async-start(bf16[128,16,1024]{2,1,0:T(8,128)(2,1)} %bitcast.54), calls=%async_computation.1 | async-start | bytes 8388608 | tf_op jit(solution)/shard_map/all_to_all | solution.py:268
  135.6 0.0 copy-start.4
  135.6 0.0 copy-start.11
  135.6 3.0 %fusion.23 = bf16[1024,1024]{1,0:T(8,128)(2,1)S(1)} fusion(bf16[512,1024]{1,0:T(8,128)(2,1)} %copy-done.12, bf16[512,1024]{1,0:T(8,128)(2,1)} %copy-done.20), kind=kOutput, calls=%fused_computation.55 | convolution fusion | flops 1073741824 | bytes 4194304 | tf_op jit(solution)/shard_map/dot_general | solution.py:226
  138.6 0.0 copy-done.4
  138.6 0.0 copy-done.11
  138.6 0.0 copy-start.21
  138.7 1.3 fusion.8
  139.9 0.0 copy-done.21
  139.9 1.3 convolution_bitcast_fusion
  141.3 2.4 pad_maximum_fusion
  143.6 91.8 %reduce_blocks.1 = (bf16[4,2,4,4,16,1024]{5,4,3,2,1,0:T(8,128)(2,1)}, f32[8,1024]{1,0:T(8,128)S(1)}) custom-call(bf16[4,2,4,4,16,1024]{5,4,3,2,1,0:T(8,128)(2,1)} %bitcast.52, bf16[4,2,4,4,8,1024]{5,4,3,2,1,0:T(8,128)(2,1)S(1)} %bitcast.51), custom_call_target="tpu_custom_call" | custom-call | tf_op jit(solution)/shard_map/reduce_blocks/pallas_call | solution.py:197
  235.4 2.0 fusion.12
  237.5 0.0 copy-done.16
  237.5 2.6 %fusion.22 = f32[512,1024]{1,0:T(8,128)} fusion(bf16[512,1024]{1,0:T(8,128)(2,1)S(1)} %copy-done.21, bf16[1024,1024]{1,0:T(8,128)(2,1)S(1)} %copy-done.16), kind=kOutput, calls=%fused_computation.54 | convolution fusion | flops 1073741824 | bytes 5242880 | tf_op jit(solution)/shard_map/dot_general | solution.py:226
  240.0 0.0 copy-done.6
  240.0 2.4 fusion.19
  242.5 0.0 all-to-all-done.1
  242.5 4.8 %fusion = f32[512,1024]{1,0:T(8,128)S(1)} fusion(bf16[2048,1024]{1,0:T(8,128)(2,1)} %bitcast.25, s32[2048]{0:T(1024)S(1)} %broadcast_select_fusion), kind=kOutput, calls=%fused_computation.19 | convolution fusion | flops 2148532224 | bytes 6299648 | tf_op jit(solution)/shard_map/dot_general | solution.py:226
  247.3 0.0 copy-done.1
  247.3 0.0 copy-done.9
  247.3 2.4 add_convert_fusion.1
  (11 shorter events, 0.1 us)
Async XLA Ops:
  0.6 117.5 %copy-start = (bf16[1024,1024]{1,0:T(8,128)(2,1)S(1)}, bf16[1024,1024]{1,0:T(8,128)(2,1)}, u32[]{:S(2)}) copy-start(bf16[1024,1024]{1,0:T(8,128)(2,1)} %param.17) | copy-start | bytes 6291460
  7.6 11.7 %copy-start.5 = (bf16[512,1024]{1,0:T(8,128)(2,1)S(1)}, bf16[512,1024]{1,0:T(8,128)(2,1)}, u32[]{:S(2)}) copy-start(bf16[512,1024]{1,0:T(8,128)(2,1)} %param.10) | copy-start | bytes 3145732
  7.6 11.7 %copy-start.15 = (s32[8]{0:T(128)S(1)}, s32[8]{0:T(128)}, u32[]{:S(2)}) copy-start(s32[8]{0:T(128)} %param.15) | copy-start | bytes 100
  7.6 78.0 %copy-start.14 = (s32[512]{0:T(512)S(1)}, s32[512]{0:T(512)}, u32[]{:S(2)}) copy-start(s32[512]{0:T(512)} %param.12) | copy-start | bytes 6148
  7.6 78.0 %copy-start.13 = (s32[512,16]{0,1:T(8,128)S(1)}, s32[512,16]{0,1:T(8,128)}, u32[]{:S(2)}) copy-start(s32[512,16]{0,1:T(8,128)} %param.11) | copy-start | bytes 98308
  7.6 104.4 %all-to-all-start = ((bf16[128,16,1024]{2,1,0:T(8,128)(2,1)}), bf16[128,16,1024]{2,1,0:T(8,128)(2,1)}, u32[]{:S(2)}, u32[]{:S(2)}) async-start(bf16[128,16,1024]{2,1,0:T(8,128)(2,1)} %bitcast.53), calls=%async_computation | async-start | bytes 8388608 | tf_op jit(solution)/shard_map/all_to_all | solution.py:243
  85.6 23.8 %copy-start.7 = (bf16[4,2,4,4,8,1024]{5,4,3,2,1,0:T(8,128)(2,1)S(1)}, bf16[4,2,4,4,8,1024]{5,4,3,2,1,0:T(8,128)(2,1)}, u32[]{:S(2)}) copy-start(bf16[4,2,4,4,8,1024]{5,4,3,2,1,0:T(8,128)(2,1)} %gather_blocks.1) | copy-start | bytes 6291460
  107.7 1.8 copy-start.2
  112.0 5.3 %copy-start.3 = (bf16[512,3584]{1,0:T(8,128)(2,1)S(1)}, bf16[512,3584]{1,0:T(8,128)(2,1)}, u32[]{:S(2)}) copy-start(bf16[512,3584]{1,0:T(8,128)(2,1)} %copy-done.2) | copy-start | bytes 11010052
  112.0 5.3 %copy-start.8 = (f32[512,1024]{1,0:T(8,128)S(1)}, f32[512,1024]{1,0:T(8,128)}, u32[]{:S(2)}) copy-start(f32[512,1024]{1,0:T(8,128)} %fusion.10) | copy-start | bytes 6291460
  117.4 1.2 copy-start.17
  117.4 1.2 copy-start.18
  117.4 1.9 copy-start.19
  119.3 3.0 %copy-start.12 = (bf16[512,1024]{1,0:T(8,128)(2,1)}, bf16[512,1024]{1,0:T(8,128)(2,1)S(1)}, u32[]{:S(2)}) copy-start(bf16[512,1024]{1,0:T(8,128)(2,1)S(1)} %multiply_convert_fusion.3) | copy-start | bytes 3145732
  122.3 1.0 copy-start.20
  124.5 4.4 %copy-start.10 = (bf16[512,1024]{1,0:T(8,128)(2,1)}, bf16[512,1024]{1,0:T(8,128)(2,1)S(1)}, u32[]{:S(2)}) copy-start(bf16[512,1024]{1,0:T(8,128)(2,1)S(1)} %multiply_convert_fusion) | copy-start | bytes 3145732
  129.0 113.5 %all-to-all-start.1 = ((bf16[128,16,1024]{2,1,0:T(8,128)(2,1)}), bf16[128,16,1024]{2,1,0:T(8,128)(2,1)}, u32[]{:S(2)}, u32[]{:S(2)}) async-start(bf16[128,16,1024]{2,1,0:T(8,128)(2,1)} %bitcast.54), calls=%async_computation.1 | async-start | bytes 8388608 | tf_op jit(solution)/shard_map/all_to_all | solution.py:268
  135.6 3.0 %copy-start.4 = (bf16[512,3584]{1,0:T(8,128)(2,1)S(1)}, bf16[512,3584]{1,0:T(8,128)(2,1)}, u32[]{:S(2)}) copy-start(bf16[512,3584]{1,0:T(8,128)(2,1)} %copy-done.2) | copy-start | bytes 11010052
  135.6 3.0 %copy-start.11 = (bf16[512,1024]{1,0:T(8,128)(2,1)S(1)}, bf16[512,1024]{1,0:T(8,128)(2,1)}, u32[]{:S(2)}) copy-start(bf16[512,1024]{1,0:T(8,128)(2,1)} %copy-done.10) | copy-start | bytes 3145732
  138.6 1.3 copy-start.21
  143.6 93.8 %copy-start.16 = (bf16[1024,1024]{1,0:T(8,128)(2,1)S(1)}, bf16[1024,1024]{1,0:T(8,128)(2,1)}, u32[]{:S(2)}) copy-start(bf16[1024,1024]{1,0:T(8,128)(2,1)} %param.16) | copy-start | bytes 6291460
  237.5 2.6 %copy-start.6 = (bf16[4,2,4,4,16,1024]{5,4,3,2,1,0:T(8,128)(2,1)S(1)}, bf16[4,2,4,4,16,1024]{5,4,3,2,1,0:T(8,128)(2,1)}, u32[]{:S(2)}) copy-start(bf16[4,2,4,4,16,1024]{5,4,3,2,1,0:T(8,128)(2,1)} %get-tuple-element.7) | copy-start | bytes 12582916
  242.5 4.8 %copy-start.1 = (f32[512,1024]{1,0:T(8,128)S(1)}, f32[512,1024]{1,0:T(8,128)}, u32[]{:S(2)}) copy-start(f32[512,1024]{1,0:T(8,128)} %fusion.12) | copy-start | bytes 6291460
  242.5 4.8 %copy-start.9 = (f32[512,1024]{1,0:T(8,128)S(1)}, f32[512,1024]{1,0:T(8,128)}, u32[]{:S(2)}) copy-start(f32[512,1024]{1,0:T(8,128)} %fusion.22) | copy-start | bytes 6291460

commit v2 on v0

v2 whole, which is shorter than its diff:
```python
import functools

import jax
import jax.numpy as jnp
from jax import lax
from jax.experimental import pallas as pl
from jax.experimental.pallas import tpu as pltpu
from jax.sharding import PartitionSpec as P

MESH = pl.DeviceIdType.MESH
F32 = jnp.float32
BF16 = jnp.bfloat16
WIDTH = 1024
LOCAL = 512
FANOUT = 16
SLOT = 16
HUB = 8
PEERS = 128
SLOTS = SLOT * PEERS
HUBS = HUB * PEERS
TABLE = LOCAL + SLOTS + HUBS
STRIDE = 37
COLS = ((0, 384), (384, 384), (768, 256))
ORDERS = (("x", "y", "z"), ("y", "z", "x"), ("z", "x", "y"))
ALL_DIMS = ("x", "core", "y", "z")


def where_am_i():
    row = lax.axis_index("row")
    col = lax.axis_index("col")
    return {"x": row // 2, "core": lax.rem(row, 2), "y": col // 4, "z": lax.rem(col, 4)}


def device_at(place):
    return (place["x"] * 2 + place["core"], place["y"] * 4 + place["z"])


def rank_of(place):
    return ((place["x"] * 2 + place["core"]) * 4 + place["y"]) * 4 + place["z"]


def shifted(place, dim, step):
    other = dict(place)
    other[dim] = lax.rem(place[dim] + step, 2 if dim == "core" else 4)
    return other


def peer_at(place, offset):
    return {
        "x": lax.rem(place["x"] + offset // 32, 4),
        "core": lax.rem(place["core"] + lax.rem(offset // 16, 2), 2),
        "y": lax.rem(place["y"] + lax.rem(offset // 4, 4), 4),
        "z": lax.rem(place["z"] + lax.rem(offset, 4), 4),
    }


def remote(src, dst, send_sem, recv_sem, peer):
    return pltpu.make_async_remote_copy(
        src_ref=src,
        dst_ref=dst,
        send_sem=send_sem,
        recv_sem=recv_sem,
        device_id=device_at(peer),
        device_id_type=MESH,
    )


def dot(a, b, ca=1, cb=0):
    return lax.dot_general(a, b, (((ca,), (cb,)), ((), ())), preferred_element_type=F32)


def loop(count, body):
    def step(i, carry):
        body(i)
        return carry

    lax.fori_loop(0, count, step, 0)


def rows(i, size):
    return pl.ds(pl.multiple_of(i * size, size), size)


def cut(part):
    start, size = COLS[part]
    return pl.ds(start, size)


def window(ref, fixed, part, dims):
    index = tuple(fixed.get(dim, slice(None)) for dim in dims)
    return ref.at[index + (slice(None), cut(part))]


class Exchange:
    def __init__(self, place, src, dst, send_sem, recv_sem):
        self.place, self.src, self.dst = place, src, dst
        self.send_sem, self.recv_sem = send_sem, recv_sem
        self.me = rank_of(place)

    def send(self, low, high):
        def body(i):
            peer = peer_at(self.place, lax.rem((low + i) * STRIDE, PEERS))
            remote(
                self.src.at[rows(rank_of(peer), SLOT)],
                self.dst.at[rows(self.me, SLOT)],
                self.send_sem,
                self.recv_sem,
                peer,
            ).start()

        loop(high - low, body)

    def wait_recv(self):
        most = pl.ds(0, SLOTS - SLOT)
        pltpu.make_async_copy(self.src.at[most], self.dst.at[most], self.recv_sem).wait()

    def wait_send(self):
        most = pl.ds(0, SLOTS - SLOT)
        pltpu.make_async_copy(self.src.at[most], self.dst.at[most], self.send_sem).wait()


class Spread:
    def __init__(self, place, out, send_sem, recv_sem):
        self.place, self.out, self.send_sem, self.recv_sem = place, out, send_sem, recv_sem

    def start(self, stage):
        place, out = self.place, self.out
        self.copies = []
        if stage == 3:
            half = out.at[:, place["core"]]
            self.copies.append(
                remote(half, half, self.send_sem.at[27], self.recv_sem.at[27], shifted(place, "core", 1))
            )
        else:
            for part, order in enumerate(ORDERS):
                dim = order[2 - stage]
                fixed = {"core": place["core"]}
                for known in order[: 3 - stage]:
                    fixed[known] = place[known]
                block = window(out, fixed, part, ALL_DIMS)
                for step in (2, 1, 3):
                    slot = (stage * 3 + part) * 3 + step - 1
                    self.copies.append(
                        remote(block, block, self.send_sem.at[slot], self.recv_sem.at[slot], shifted(place, dim, step))
                    )
        for copy in self.copies:
            copy.start()

    def finish(self):
        for copy in self.copies:
            copy.wait()


class Reduce:
    def __init__(self, place, sources, bufs, finals, send_sem, recv_sem):
        self.place, self.sources, self.bufs, self.finals = place, sources, bufs, finals
        self.send_sem, self.recv_sem = send_sem, recv_sem

    def start_core(self):
        partner = shifted(self.place, "core", 1)
        self.copies = []
        for i, src in enumerate(self.sources):
            copy = remote(
                src.at[:, partner["core"]], self.bufs[i][0], self.send_sem.at[i], self.recv_sem.at[i], partner
            )
            copy.start()
            self.copies.append(copy)

    def finish_core(self):
        core = self.place["core"]
        for i, src in enumerate(self.sources):
            self.copies[i].wait()
            got, total = self.bufs[i][0], self.bufs[i][1]

            def add(t, src=src, got=got, total=total):
                x, y, z = t // 16, lax.rem(t // 4, 4), lax.rem(t, 4)
                total[x, y, z] = (src[x, core, y, z].astype(F32) + got[x, y, z].astype(F32)).astype(BF16)

            loop(64, add)

    def start(self, stage):
        place, n = self.place, len(self.sources)
        self.started = []
        for part, order in enumerate(ORDERS):
            dim = order[stage]
            dims = [d for d in "xyz" if d not in order[:stage]]
            for i in range(n):
                held, came = self.bufs[i][1 + 2 * stage], self.bufs[i][2 + 2 * stage]
                mine = []
                for step in (2, 1, 3):
                    peer = shifted(place, dim, step)
                    slot = n + ((stage * 3 + part) * n + i) * 3 + step - 1
                    dst = came.at[(step - 1,) + (slice(None),) * (len(dims) - 1) + (slice(None), cut(part))]
                    copy = remote(
                        window(held, {dim: peer[dim]}, part, dims),
                        dst,
                        self.send_sem.at[slot],
                        self.recv_sem.at[slot],
                        peer,
                    )
                    copy.start()
                    mine.append(copy)
                self.started.append((part, i, dims, dim, held, came, mine))

    def finish(self, stage):
        place = self.place
        for part, i, dims, dim, held, came, mine in self.started:
            for copy in mine:
                copy.wait()
            cols = cut(part)
            rest = [d for d in dims if d != dim]

            def fold(t, part=part, i=i, dims=dims, dim=dim, held=held, came=came, cols=cols, rest=rest):
                at = {dim: place[dim]}
                if len(rest) == 2:
                    at[rest[0]], at[rest[1]] = t // 4, lax.rem(t, 4)
                elif len(rest) == 1:
                    at[rest[0]] = t
                spot = tuple(at[d] for d in rest)
                total = held[tuple(at[d] for d in dims) + (slice(None), cols)].astype(F32)
                for k in range(3):
                    total += came[(k,) + spot + (slice(None), cols)].astype(F32)
                if rest:
                    self.bufs[i][3 + 2 * stage][spot + (slice(None), cols)] = total.astype(BF16)
                else:
                    self.finals[i](cols, total)

            if rest:
                loop(4 ** len(rest), fold)
            else:
                fold(0)


def sage_kernel(
    features,
    neighbours_t,
    degrees,
    send_rows,
    send_count,
    hub_rows,
    bias,
    w_self_hbm,
    w_neigh_hbm,
    cotangent_hbm,
    hidden,
    grad_x,
    grads_all,
    w_self,
    w_neigh,
    cotangent,
    picks_t,
    hub_picks,
    outgoing,
    arrived,
    returned,
    hub_blocks,
    hub_table,
    nbr_wide,
    counts_t,
    counts,
    inv_deg,
    total,
    pre_self,
    aggregate,
    d_pre,
    d_agg,
    grads_own,
    hubs_own,
    hub_back,
    *rest,
):
    bufs = [rest[0:7], rest[7:14]]
    (
        local_sem,
        fwd_send,
        fwd_recv,
        bwd_send,
        bwd_recv,
        hub_send,
        hub_recv,
        red_send,
        red_recv,
        all_send,
        all_recv,
    ) = rest[14:]
    place = where_am_i()
    me = rank_of(place)
    barrier = pltpu.get_barrier_semaphore()

    def greet(i):
        peer = peer_at(place, i + 1)
        pl.semaphore_signal(barrier, inc=1, device_id=device_at(peer), device_id_type=MESH)

    loop(PEERS - 1, greet)
    loads = [
        pltpu.make_async_copy(src, dst, local_sem.at[i])
        for i, (src, dst) in enumerate(((w_self_hbm, w_self), (w_neigh_hbm, w_neigh), (cotangent_hbm, cotangent)))
    ]
    for load in loads:
        load.start()

    owner = lax.broadcasted_iota(jnp.int32, (PEERS, SLOTS), 1) // SLOT
    widen = (owner == lax.broadcasted_iota(jnp.int32, (PEERS, SLOTS), 0)).astype(F32).astype(BF16)
    count = jnp.broadcast_to(send_count[...], (8, PEERS)).astype(F32).astype(BF16)
    count_wide = dot(count, widen)[0:1]
    place_in = lax.rem(lax.broadcasted_iota(jnp.int32, (1, SLOTS), 1), SLOT)
    live_row = jnp.where(place_in.astype(F32) < count_wide, send_rows[...], -1)

    def pick(i):
        row = lax.broadcasted_iota(jnp.int32, (64, SLOTS), 0) + i * 64
        picks_t[rows(i, 64)] = (row == live_row).astype(F32).astype(BF16)

    loop(LOCAL // 64, pick)

    def fill(i):
        outgoing[rows(i, 512)] = dot(picks_t[:, rows(i, 512)], features[...], 0, 0).astype(BF16)

    loop(SLOTS // 512, fill)
    which = lax.broadcasted_iota(jnp.int32, (SLOT, LOCAL), 0)
    chosen = jnp.zeros((SLOT, LOCAL), jnp.int32)
    for h in range(HUB):
        chosen = jnp.where(lax.rem(which, HUB) == h, hub_rows[h], chosen)
    hub_picks[...] = (chosen == lax.broadcasted_iota(jnp.int32, (SLOT, LOCAL), 1)).astype(F32).astype(BF16)
    own_hubs = dot(hub_picks[...], features[...])[:HUB]
    hub_blocks[place["x"], place["core"], place["y"], place["z"]] = own_hubs.astype(BF16)
    arrived[rows(me, SLOT)] = jnp.zeros((SLOT, WIDTH), BF16)
    returned[rows(me, SLOT)] = jnp.zeros((SLOT, WIDTH), BF16)

    forward = Exchange(place, outgoing, arrived, fwd_send, fwd_recv)
    backward = Exchange(place, outgoing, returned, bwd_send, bwd_recv)
    hub_spread = Spread(place, hub_blocks, hub_send, hub_recv)
    pl.semaphore_wait(barrier, PEERS - 1)

    live = lax.broadcasted_iota(jnp.int32, (FANOUT, LOCAL), 0) < degrees[...]
    target = jnp.where(live, neighbours_t[...], -1)
    for j in range(FANOUT):
        nbr_wide[j] = jnp.broadcast_to(target[j : j + 1], (8, LOCAL))
    inv_deg[...] = (1.0 / jnp.broadcast_to(degrees[...], (128, LOCAL)).astype(F32)).T

    def count_block(b):
        def strip(i):
            base = b * 128 + i * 32
            sums = [jnp.zeros((8, LOCAL), F32) for _ in range(4)]
            ids = [lax.broadcasted_iota(jnp.int32, (8, LOCAL), 0) + (base + 8 * g) for g in range(4)]
            for j in range(FANOUT):
                named = nbr_wide[j]
                for g in range(4):
                    sums[g] = sums[g] + jnp.where(named == ids[g], 1.0, 0.0)
            counts_t[pl.ds(pl.multiple_of(base, 32), 32)] = jnp.concatenate(sums, 0).astype(BF16)

        loop(4, strip)
        counts[:, rows(b, 128)] = counts_t[rows(b, 128)].astype(F32).T.astype(BF16)

    blocks = TABLE // 128
    for stage in range(4):
        hub_spread.start(stage)
        forward.send(1 + stage * 32, min(1 + (stage + 1) * 32, PEERS))
        first = blocks * stage // 4
        loop(blocks * (stage + 1) // 4 - first, lambda i, first=first: count_block(first + i))
        hub_spread.finish()

    def to_table(x):
        hub_table[rows(x, 256)] = hub_blocks[x].astype(F32).reshape(256, WIDTH).astype(BF16)

    loop(4, to_table)
    loads[0].wait()

    def before(i):
        cols = rows(i, 256)
        pre_self[:, cols] = dot(features[...], w_self[:, cols]) + bias[:, cols]
        total[:, cols] = dot(counts[:, :LOCAL], features[:, cols]) + dot(
            counts[:, LOCAL + SLOTS :], hub_table[:, cols]
        )

    loop(4, before)
    loads[1].wait()
    loads[2].wait()
    forward.wait_recv()

    def with_slots(i):
        cols = rows(i, 256)
        total[:, cols] += dot(counts[:, LOCAL : LOCAL + SLOTS], arrived[:, cols])

    loop(4, with_slots)

    def mean(i):
        scale = jnp.concatenate([inv_deg[rows(i, 64)]] * (WIDTH // 128), 1)
        aggregate[rows(i, 64)] = (total[rows(i, 64)] * scale).astype(BF16)

    loop(LOCAL // 64, mean)

    def act(i):
        m = rows(i, 128)
        pre = pre_self[m] + dot(aggregate[m], w_neigh[...])
        sigmoid = jax.nn.sigmoid(pre)
        hidden[m] = (pre * sigmoid).astype(BF16)
        slope = sigmoid * (1.0 + pre * (1.0 - sigmoid))
        d_pre[m] = (cotangent[m].astype(F32) * slope).astype(BF16)

    loop(LOCAL // 128, act)

    def d_mean(i):
        m = rows(i, 128)
        scale = jnp.concatenate([inv_deg[m]] * (WIDTH // 128), 1)
        d_agg[m] = (dot(d_pre[m], w_neigh[...], 1, 1) * scale).astype(BF16)

    loop(LOCAL // 128, d_mean)
    forward.wait_send()

    def d_slots(i):
        m = rows(i, 512)
        outgoing[m] = dot(counts_t[pl.ds(pl.multiple_of(LOCAL + i * 512, 512), 512)], d_agg[...]).astype(BF16)

    loop(SLOTS // 512, d_slots)
    backward.send(1, 25)

    def grads_to(first, source):
        def body(i):
            block = dot(source[:, rows(i, 512)], d_pre[...], 0, 0).astype(BF16)
            grads_own[first + i] = block.reshape(2, 4, 4, SLOT, WIDTH)

        loop(2, body)

    grads_to(0, features)
    grads_to(2, aggregate)

    def d_hubs(i):
        base = LOCAL + SLOTS + i * 256
        block = dot(counts_t[pl.ds(pl.multiple_of(base, 256), 256)], d_agg[...])
        hubs_own[i] = block.reshape(2, 4, 4, HUB, WIDTH).astype(BF16)

    loop(4, d_hubs)

    def keep_grads(cols, value):
        grads_all[place["x"], place["core"], place["y"], place["z"], :, cols] = value.astype(BF16)

    def keep_hubs(cols, value):
        hub_back[:, cols] = value

    reduce = Reduce(place, (grads_own, hubs_own), bufs, (keep_grads, keep_hubs), red_send, red_recv)
    spread = Spread(place, grads_all, all_send, all_recv)
    reduce.start_core()
    backward.send(25, 42)

    def own_grad(i):
        m = rows(i, 128)
        total[m] = dot(d_pre[m], w_self[...], 1, 1) + dot(counts_t[m], d_agg[...])

    loop(LOCAL // 128, own_grad)
    reduce.finish_core()
    reduce.start(0)
    backward.send(42, 62)
    reduce.finish(0)
    reduce.start(1)
    backward.send(62, 80)
    reduce.finish(1)
    reduce.start(2)
    backward.send(80, 96)
    reduce.finish(2)
    spread.start(0)
    backward.send(96, 112)
    spread.finish()
    spread.start(1)
    backward.send(112, PEERS)
    spread.finish()
    spread.start(2)

    high = hub_back[...].astype(BF16)
    low = (hub_back[...] - high.astype(F32)).astype(BF16)
    both = jnp.concatenate([high.astype(F32), low.astype(F32)], 0).astype(BF16)
    backward.wait_recv()

    def final(i):
        cols = rows(i, 256)
        value = total[:, cols] + dot(picks_t[...], returned[:, cols])
        total[:, cols] = value

    loop(4, final)
    grad_x[...] = (total[...] + dot(hub_picks[...], both, 0, 0)).astype(BF16)
    spread.finish()
    spread.start(3)
    backward.wait_send()
    spread.finish()


def on_device(
    features, neighbours, degrees, send_rows, send_count, hub_rows, w_self, w_neigh, bias_term, cotangent
):
    vmem = pl.BlockSpec(memory_space=pltpu.VMEM)
    hbm = pl.BlockSpec(memory_space=pl.ANY)
    wide = (WIDTH,)

    def buf(*shape, kind=BF16):
        return pltpu.VMEM(shape, kind)

    reduce_bufs = []
    for size in (SLOT, HUB):
        for shape in ((4, 4, 4), (4, 4, 4), (3, 4, 4), (4, 4), (3, 4), (4,), (3,)):
            reduce_bufs.append(buf(*shape, size, WIDTH))
    dma = pltpu.SemaphoreType.DMA
    hidden, grad_x, grads = pl.pallas_call(
        sage_kernel,
        out_shape=(
            jax.ShapeDtypeStruct((LOCAL, WIDTH), BF16),
            jax.ShapeDtypeStruct((LOCAL, WIDTH), BF16),
            jax.ShapeDtypeStruct((4, 2, 4, 4, SLOT, WIDTH), BF16),
        ),
        in_specs=[vmem] * 5 + [pl.BlockSpec(memory_space=pltpu.SMEM)] + [vmem] + [hbm] * 3,
        out_specs=[vmem] * 3,
        scratch_shapes=[
            buf(WIDTH, WIDTH),
            buf(WIDTH, WIDTH),
            buf(LOCAL, WIDTH),
            buf(LOCAL, SLOTS),
            buf(SLOT, LOCAL),
            buf(SLOTS, WIDTH),
            buf(SLOTS, WIDTH),
            buf(SLOTS, WIDTH),
            buf(4, 2, 4, 4, HUB, WIDTH),
            buf(HUBS, WIDTH),
            buf(FANOUT, 8, LOCAL, kind=jnp.int32),
            buf(TABLE, LOCAL),
            buf(LOCAL, TABLE),
            buf(LOCAL, 128, kind=F32),
            buf(LOCAL, WIDTH, kind=F32),
            buf(LOCAL, WIDTH, kind=F32),
            buf(LOCAL, WIDTH),
            buf(LOCAL, WIDTH),
            buf(LOCAL, WIDTH),
            buf(4, 2, 4, 4, SLOT, WIDTH),
            buf(4, 2, 4, 4, HUB, WIDTH),
            buf(HUB, WIDTH, kind=F32),
            *reduce_bufs,
            dma((3,)),
            dma,
            dma,
            dma,
            dma,
            dma((28,)),
            dma((28,)),
            dma((56,)),
            dma((56,)),
            dma((28,)),
            dma((28,)),
        ],
        compiler_params=pltpu.CompilerParams(
            collective_id=0, has_side_effects=True, vmem_limit_bytes=67043328
        ),
        name="sage",
    )(
        features,
        neighbours.T,
        degrees[None, :],
        send_rows,
        send_count,
        hub_rows,
        bias_term[None, :],
        w_self,
        w_neigh,
        cotangent,
    )
    grads = grads.reshape(2 * WIDTH, WIDTH)
    return hidden, grad_x, grads[:WIDTH], grads[WIDTH:]


def solution(mesh):
    split = P(("row", "col"), None)
    in_specs = (split, split, P(("row", "col")), split, split, P(("row", "col")), P(), P(), P(), split)
    out_specs = (split, split, P(), P())
    return jax.shard_map(on_device, mesh=mesh, in_specs=in_specs, out_specs=out_specs, check_vma=False)
```

time: 959 us -> 181 us (0.19)
  waiting for transfers between devices: 540 us -> 0 us
  Pallas kernels: 0 us -> 171 us
  blocking collectives: 148 us -> 0 us
  other arithmetic: 117 us -> 0 us
  local copies, waits for them, and re-layouts: 90.1 us -> 7.73 us
  matrix products: 30.2 us -> 0 us
  starting transfers between devices: 18.4 us -> 0 us
  between operations: 14.3 us -> 0.65 us
    reduce_scatter x1 -> x0, waiting for transfers between devices: 476 us -> none  [on_device(): lax.psum_scatter(d_hubs, ('row', 'col'), scatter_dimension=0, tiled=True)]
    pallas_call x0 -> x1, Pallas kernels: none -> 171 us  [on_device(): pl.pallas_call(sage_kernel, out_shape=(jax.ShapeDtypeStruct((LOCAL, WIDTH...]
    psum x1 -> x0, blocking collectives: 148 us -> none  [on_device(): grad_self, grad_neigh = lax.psum((self_part, neigh_part), ('row', 'col'))]
    scatter-add x3 -> x0, other arithmetic: 102 us -> none  [the longest x1 77.1 us: spread_tile(): d_table.at[target.reshape(-1)]]
    all_gather x1 -> x0, waiting for transfers between devices: 64.1 us -> none  [on_device(): all_hubs = lax.all_gather(own_hubs, ('row', 'col'), axis=0, tiled=True)]
    gather x3 -> x0, local copies, waits for them, and re-layouts: 59.5 us -> none  [the longest x1 44.7 us: gather_tile(): picked = src_table[neighbours]]
    dot_general x7 -> x0, matrix products: 30.2 us -> none  [the longest x1 8.64 us: gather_tile(): jnp.einsum('nf,nfd->nd', tile_live, picked, preferred_element_type=jnp.fl...]
    all_to_all x2 -> x0, starting transfers between devices: 18.3 us -> none  [the longest x1 11.7 us: on_device(): lax.all_to_all(outgoing, ('row', 'col'), split_axis=0, concat_axis=0, til...]
  transfers between devices with their start and end apart: 4 -> 0, of which waited for: 2 -> 0; matrix products, arithmetic and copies ran while one was open for 7% -> 0% of each run, Pallas kernels for 0% -> 0%
where the time goes in v2:
time: 181 us; the launch traced here: 179 us
  Pallas kernels  171 us (94%)
  local copies, waits for them, and re-layouts  7.73 us (4%)
    pallas_call x1, Pallas kernels, on_device(): pl.pallas_call(sage_kernel, out_shape=(jax.ShapeDtypeStruct((LOCAL, WIDTH...  171 us
    slice x1, local copies, waits for them, and re-layouts, on_device(): return (hidden, grad_x, grads[:WIDTH], grads[WIDTH:])  5.16 us

profile of v2, /device:TPU:0, one launch (start us, length us, event | category | flops | bytes accessed | tf_op | source)
XLA Modules:
  0.0 179.2 jit_solution(3833196864285574332)
XLA Ops:
  0.6 170.8 %sage.1 = (bf16[512,1024]{1,0:T(8,128)(2,1)}, bf16[512,1024]{1,0:T(8,128)(2,1)}, bf16[4,2,4,4,16,1024]{5,4,3,2,1,0:T(8,128)(2,1)}) custom-call(bf16[512,1024]{1,0:T(8,128)(2,1)} %features.1, s32[16,512]{1,0:T(8,128)} %bitcast.7, s32[1,512]{1,0:T(1,128)} %bitcast.9, s32[1,2048]{1,0:T(1,128)} %send_rows.1, s32[1,128]{1,0:T(1,128)} %send_count.1, s32[8]{0:T(128)} %hub_rows.1, ...), custom_call_target="tpu_custom_call" | custom-call | tf_op jit(solution)/shard_map/sage/pallas_call | solution.py:501
  171.4 0.0 copy-start.1
  171.4 5.2 %fusion = (bf16[2,2,4,4,16,1024]{5,4,3,2,1,0:T(8,128)(2,1)}, bf16[2,2,4,4,16,1024]{5,4,3,2,1,0:T(8,128)(2,1)}) fusion(bf16[4,2,4,4,16,1024]{5,4,3,2,1,0:T(8,128)(2,1)} %get-tuple-element.9), kind=kLoop, calls=%fused_computation | loop fusion | bytes 8388608 | tf_op jit(solution)/shard_map/slice | solution.py:563
  176.6 0.0 copy-start
  176.6 0.0 copy-done.1
  176.6 1.0 copy.16
  177.6 0.6 copy-done
  178.2 1.0 copy.17
Async XLA Ops:
  171.4 5.2 %copy-start.1 = (bf16[512,1024]{1,0:T(8,128)(2,1)S(1)}, bf16[512,1024]{1,0:T(8,128)(2,1)}, u32[]{:S(2)}) copy-start(bf16[512,1024]{1,0:T(8,128)(2,1)} %get-tuple-element.16) | copy-start | bytes 3145732
  176.6 1.6 copy-start

commit v3 on v2

v3 whole, which is shorter than its diff:
```python
import functools

import jax
import jax.numpy as jnp
from jax import lax
from jax.experimental import pallas as pl
from jax.experimental.pallas import tpu as pltpu
from jax.sharding import PartitionSpec as P

MESH = pl.DeviceIdType.MESH
F32 = jnp.float32
BF16 = jnp.bfloat16
WIDTH = 1024
LOCAL = 512
FANOUT = 16
SLOT = 16
HUB = 8
PEERS = 128
SLOTS = SLOT * PEERS
HUBS = HUB * PEERS
TABLE = LOCAL + SLOTS + HUBS
XYZ, YZX, ZXY = ("x", "y", "z"), ("y", "z", "x"), ("z", "x", "y")
HUB_PIECES = ((0, 0, 384, XYZ), (0, 384, 384, YZX), (0, 768, 256, ZXY))
GRAD_PIECES = ((0, 0, 640, XYZ), (1, 0, 640, YZX), (0, 640, 384, ZXY), (1, 640, 384, ZXY))
SUM_ORDERS = (XYZ, YZX, ZXY)


def where_am_i():
    row = lax.axis_index("row")
    col = lax.axis_index("col")
    return {"x": row // 2, "core": lax.rem(row, 2), "y": col // 4, "z": lax.rem(col, 4)}


def device_at(place):
    return (place["x"] * 2 + place["core"], place["y"] * 4 + place["z"])


def rank_of(place):
    return ((place["x"] * 2 + place["core"]) * 4 + place["y"]) * 4 + place["z"]


def shifted(place, dim, step):
    other = dict(place)
    other[dim] = lax.rem(place[dim] + step, 2 if dim == "core" else 4)
    return other


def message_order():
    left = [(x, c, y, z) for x in range(4) for y in range(4) for z in range(4) for c in range(2)][1:]
    load = [0] * 6
    order = []

    def after(offset):
        new = list(load)
        for axis, step in enumerate((offset[0], offset[2], offset[3])):
            if step in (1, 2):
                new[2 * axis] += 1
            if step in (2, 3):
                new[2 * axis + 1] += 1
        return new

    def unevenness(offset):
        new = after(offset)
        mean = sum(new) / 6
        return (max(new) - min(new), sum((v - mean) ** 2 for v in new), [(7 * v) % 4 for v in offset])

    while left:
        best = min(left, key=unevenness)
        left.remove(best)
        load[:] = after(best)
        order.append(best)
    return order


ORDER = message_order()


class Peers:
    def __init__(self, place):
        xs = [lax.rem(place["x"] + d, 4) for d in range(4)]
        cores = [place["core"], 1 - place["core"]]
        ys = [lax.rem(place["y"] + d, 4) for d in range(4)]
        zs = [lax.rem(place["z"] + d, 4) for d in range(4)]
        self.rows = [[x * 2 + c for c in cores] for x in xs]
        self.cols = [[y * 4 + z for z in zs] for y in ys]

    def device(self, offset):
        return (self.rows[offset[0]][offset[1]], self.cols[offset[2]][offset[3]])

    def rank(self, offset):
        row, col = self.device(offset)
        return row * 16 + col


def remote(src, dst, send_sem, recv_sem, peer):
    return pltpu.make_async_remote_copy(
        src_ref=src,
        dst_ref=dst,
        send_sem=send_sem,
        recv_sem=recv_sem,
        device_id=device_at(peer),
        device_id_type=MESH,
    )


def dot(a, b, ca=1, cb=0):
    return lax.dot_general(a, b, (((ca,), (cb,)), ((), ())), preferred_element_type=F32)


def loop(count, body):
    def step(i, carry):
        body(i)
        return carry

    lax.fori_loop(0, count, step, 0)


def rows(i, size):
    return pl.ds(pl.multiple_of(i * size, size), size)


PLANE = [(i, j) for i in range(4) for j in range(4)][1:]


def in_plane(place, order, steps):
    return shifted(shifted(place, order[1], steps[0]), order[2], steps[1])


def wait_for(ref, slot, send_sem, recv_sem):
    for sem in (send_sem, recv_sem):
        pltpu.make_async_copy(ref, ref, sem.at[slot]).wait()


class Exchange:
    def __init__(self, peers, me, src, dst, send_sem, recv_sem):
        self.peers, self.me, self.src, self.dst = peers, me, src, dst
        self.send_sem, self.recv_sem = send_sem, recv_sem
        self.sent = 0

    def send(self, count=PEERS):
        for offset in ORDER[self.sent : self.sent + count]:
            pltpu.make_async_remote_copy(
                src_ref=self.src.at[rows(self.peers.rank(offset), SLOT)],
                dst_ref=self.dst.at[rows(self.me, SLOT)],
                send_sem=self.send_sem,
                recv_sem=self.recv_sem,
                device_id=self.peers.device(offset),
                device_id_type=MESH,
            ).start()
        self.sent += count

    def wait_recv(self):
        most = pl.ds(0, SLOTS - SLOT)
        pltpu.make_async_copy(self.src.at[most], self.dst.at[most], self.recv_sem).wait()

    def wait_send(self):
        most = pl.ds(0, SLOTS - SLOT)
        pltpu.make_async_copy(self.src.at[most], self.dst.at[most], self.send_sem).wait()


class Spread:
    def __init__(self, place, outs, orders, sizes, send_sem, recv_sem):
        self.place, self.outs, self.orders, self.sizes = place, outs, orders, sizes
        self.send_sem, self.recv_sem = send_sem, recv_sem
        self.passed = []

    def send(self, piece, spot, kind, peer):
        block = self.outs[piece].at[(self.place["core"],) + spot]
        slot = piece * 10 + kind
        copy = remote(block, block, self.send_sem.at[slot], self.recv_sem.at[slot], peer)
        copy.start()
        return copy

    def hand_over(self, piece, spot, kind):
        self.passed.append(self.send(piece, spot, kind, shifted(self.place, "core", 1)))

    def start_plane(self):
        for steps in PLANE:
            for piece, order in enumerate(self.orders):
                spot = tuple(self.place[d] for d in order)
                self.send(piece, spot, 9, in_plane(self.place, order, steps))

    def finish_plane(self):
        for piece, size in enumerate(self.sizes):
            wait_for(size.at[:, :, : self.outs[piece].shape[-1]], piece * 10 + 9, self.send_sem, self.recv_sem)

    def start_last(self):
        self.copies = []
        for piece, order in enumerate(self.orders):
            spot = (self.place[order[0]],)
            up = self.send(piece, spot, 0, shifted(self.place, order[0], 1))
            down = self.send(piece, spot, 1, shifted(self.place, order[0], 3))
            self.copies.append((up, down))
        for piece, order in enumerate(self.orders):
            self.hand_over(piece, (self.place[order[0]],), 4)

    def relay(self):
        relayed = []
        for piece, order in enumerate(self.orders):
            at, (up, down) = self.place[order[0]], self.copies[piece]
            below, above = lax.rem(at + 3, 4), lax.rem(at + 1, 4)
            up.wait()
            first = self.send(piece, (below, pl.ds(0, 2)), 2, shifted(self.place, order[0], 1))
            self.hand_over(piece, (below,), 5)
            down.wait()
            second = self.send(piece, (above, pl.ds(2, 2)), 3, shifted(self.place, order[0], 3))
            self.hand_over(piece, (above,), 6)
            relayed.append((first, second))
        self.copies = relayed

    def finish_last(self):
        for piece, order in enumerate(self.orders):
            far = lax.rem(self.place[order[0]] + 2, 4)
            for half, copy in enumerate(self.copies[piece]):
                copy.wait()
                self.hand_over(piece, (far, pl.ds(2 * half, 2)), 7 + half)

    def finish_cores(self):
        for copy in self.passed:
            copy.wait()


class Reduce:
    def __init__(self, place, own, got, held, half, near, came, final, send_sem, recv_sem):
        self.place, self.own, self.got, self.held = place, own, got, held
        self.half, self.near, self.came, self.final = half, near, came, final
        self.send_sem, self.recv_sem = send_sem, recv_sem

    def send(self, src, dst, slot, peer):
        copy = remote(src, dst, self.send_sem.at[slot], self.recv_sem.at[slot], peer)
        copy.start()
        return copy

    def start_core(self, source):
        partner = shifted(self.place, "core", 1)
        return self.send(self.own[source].at[partner["core"]], self.got[source], source, partner)

    def finish_core(self, source, copy):
        core = self.place["core"]
        own, got, held = self.own[source], self.got[source], self.held[0][source]
        copy.wait()

        def add(t):
            a, b = t // 4, lax.rem(t, 4)
            held[a, b] = (own[core, a, b].astype(F32) + got[a, b].astype(F32)).astype(BF16)

        loop(16, add)

    def start_halves(self):
        self.copies = []
        for source, order in enumerate(SUM_ORDERS):
            far = lax.rem(self.place[order[0]] + 2, 4)
            for i, step in enumerate((1, 3)):
                part = self.held[0][source].at[far, pl.ds(2 * i, 2)]
                peer = shifted(self.place, order[0], step)
                self.copies.append(self.send(part, self.half[source].at[i], 3 + source * 2 + i, peer))

    def finish_halves(self):
        for source, order in enumerate(SUM_ORDERS):
            held, half = self.held[0][source], self.half[source]
            for i, step in enumerate((1, 3)):
                self.copies[source * 2 + i].wait()
                at = lax.rem(self.place[order[0]] + step, 4)
                for b in range(2):
                    value = held[at, 2 * i + b].astype(F32) + half[i, b].astype(F32)
                    held[at, 2 * i + b] = value.astype(BF16)

    def start_near(self):
        self.copies = []
        for source, order in enumerate(SUM_ORDERS):
            for i, step in enumerate((1, 3)):
                peer = shifted(self.place, order[0], step)
                part = self.held[0][source].at[peer[order[0]]]
                self.copies.append(self.send(part, self.near[source].at[i], 9 + source * 2 + i, peer))

    def finish_near(self):
        for source, order in enumerate(SUM_ORDERS):
            for i in range(2):
                self.copies[source * 2 + i].wait()
            held, near, at = self.held[0][source], self.near[source], self.place[order[0]]

            def fold(b, source=source, held=held, near=near, at=at):
                value = held[at, b].astype(F32) + near[0, b].astype(F32) + near[1, b].astype(F32)
                self.held[1][source][b] = value.astype(BF16)

            loop(4, fold)

    def start_plane(self):
        for k, steps in enumerate(PLANE):
            for source, order in enumerate(SUM_ORDERS):
                peer = in_plane(self.place, order, steps)
                part = self.held[1][source].at[peer[order[1]], peer[order[2]]]
                self.send(part, self.came[source].at[k], 15 + source, peer)

    def finish_plane(self):
        for source in range(3):
            wait_for(self.came[source], 15 + source, self.send_sem, self.recv_sem)
        for source, order in enumerate(SUM_ORDERS):
            value = self.held[1][source][self.place[order[1]], self.place[order[2]]].astype(F32)
            for k in range(15):
                value += self.came[source][k].astype(F32)
            self.final(source, value)


def sage_kernel(
    features,
    neighbours_t,
    degrees,
    send_rows,
    send_count,
    hub_rows,
    bias,
    w_self_hbm,
    w_neigh_hbm,
    cotangent_hbm,
    hidden_hbm,
    grad_x_hbm,
    all_self,
    all_neigh,
    hidden,
    grad_x,
    w_self,
    w_neigh,
    w_neigh_t,
    cotangent,
    picks_t,
    hub_picks,
    outgoing,
    arrived,
    returned,
    hub_table,
    nbr_wide,
    counts_t,
    counts,
    inv_deg,
    total,
    pre_self,
    aggregate,
    d_pre,
    d_agg,
    hub_back,
    *rest,
):
    groups, at = [], 0
    for size in (3, 4, 3, 3, 3, 3, 3, 3, 3):
        groups.append(rest[at : at + size])
        at += size
    hub_parts, all_parts, own, got, *held, half, near, came = groups
    (
        local_sem,
        out_sem,
        fwd_send,
        fwd_recv,
        bwd_send,
        bwd_recv,
        hub_send,
        hub_recv,
        red_send,
        red_recv,
        all_send,
        all_recv,
    ) = rest[28:]
    place = where_am_i()
    me = rank_of(place)
    barrier = pltpu.get_barrier_semaphore()

    peers = Peers(place)
    for offset in sorted(ORDER, key=lambda o: -sum(min(o[i], 4 - o[i]) for i in (0, 2, 3))):
        pl.semaphore_signal(barrier, inc=1, device_id=peers.device(offset), device_id_type=MESH)
    loads = [
        pltpu.make_async_copy(src, dst, local_sem.at[i])
        for i, (src, dst) in enumerate(((w_self_hbm, w_self), (w_neigh_hbm, w_neigh), (cotangent_hbm, cotangent)))
    ]
    for load in loads:
        load.start()

    owner = lax.broadcasted_iota(jnp.int32, (PEERS, SLOTS), 1) // SLOT
    widen = (owner == lax.broadcasted_iota(jnp.int32, (PEERS, SLOTS), 0)).astype(F32).astype(BF16)
    count = jnp.broadcast_to(send_count[...], (8, PEERS)).astype(F32).astype(BF16)
    count_wide = dot(count, widen)[0:1]
    place_in = lax.rem(lax.broadcasted_iota(jnp.int32, (1, SLOTS), 1), SLOT)
    live_row = jnp.where(place_in.astype(F32) < count_wide, send_rows[...], -1)

    def pick(i):
        row = lax.broadcasted_iota(jnp.int32, (64, SLOTS), 0) + i * 64
        picks_t[rows(i, 64)] = (row == live_row).astype(F32).astype(BF16)

    loop(LOCAL // 64, pick)

    def fill(i):
        outgoing[rows(i, 512)] = dot(picks_t[:, rows(i, 512)], features[...], 0, 0).astype(BF16)

    loop(SLOTS // 512, fill)
    which = lax.broadcasted_iota(jnp.int32, (SLOT, LOCAL), 0)
    chosen = jnp.zeros((SLOT, LOCAL), jnp.int32)
    for h in range(HUB):
        chosen = jnp.where(lax.rem(which, HUB) == h, hub_rows[h], chosen)
    hub_picks[...] = (chosen == lax.broadcasted_iota(jnp.int32, (SLOT, LOCAL), 1)).astype(F32).astype(BF16)
    own_hubs = dot(hub_picks[...], features[...])[:HUB]
    for part, (_, start, size, order) in zip(hub_parts, HUB_PIECES):
        part[(place["core"],) + tuple(place[d] for d in order)] = own_hubs[:, start : start + size].astype(BF16)
    arrived[rows(me, SLOT)] = jnp.zeros((SLOT, WIDTH), BF16)
    returned[rows(me, SLOT)] = jnp.zeros((SLOT, WIDTH), BF16)

    forward = Exchange(peers, me, outgoing, arrived, fwd_send, fwd_recv)
    backward = Exchange(peers, me, outgoing, returned, bwd_send, bwd_recv)
    hub_spread = Spread(place, hub_parts, [p[3] for p in HUB_PIECES], [came[0]] * 3, hub_send, hub_recv)
    pl.semaphore_wait(barrier, PEERS - 1)

    live = lax.broadcasted_iota(jnp.int32, (FANOUT, LOCAL), 0) < degrees[...]
    target = jnp.where(live, neighbours_t[...], -1)
    for j in range(FANOUT):
        nbr_wide[j] = jnp.broadcast_to(target[j : j + 1], (8, LOCAL))
    inv_deg[...] = (1.0 / jnp.broadcast_to(degrees[...], (128, LOCAL)).astype(F32)).T

    def count_block(b):
        def strip(i):
            base = b * 128 + i * 32
            sums = [jnp.zeros((8, LOCAL), F32) for _ in range(4)]
            ids = [lax.broadcasted_iota(jnp.int32, (8, LOCAL), 0) + (base + 8 * g) for g in range(4)]
            for j in range(FANOUT):
                named = nbr_wide[j]
                for g in range(4):
                    sums[g] = sums[g] + jnp.where(named == ids[g], 1.0, 0.0)
            counts_t[pl.ds(pl.multiple_of(base, 32), 32)] = jnp.concatenate(sums, 0).astype(BF16)

        loop(4, strip)
        counts[:, rows(b, 128)] = counts_t[rows(b, 128)].astype(F32).T.astype(BF16)

    def count_blocks(low, high):
        loop(high - low, lambda i: count_block(low + i))

    hub_spread.start_plane()
    forward.send(30)
    count_blocks(0, 14)
    hub_spread.finish_plane()
    hub_spread.start_last()
    forward.send(40)
    count_blocks(14, 21)
    hub_spread.relay()
    forward.send()
    count_blocks(21, 28)
    hub_spread.finish_last()

    loads[1].wait()

    def turn(i):
        w_neigh_t[:, rows(i, 128)] = w_neigh[rows(i, 128)].astype(F32).T.astype(BF16)

    loop(WIDTH // 128, turn)
    hub_spread.finish_cores()

    def assemble(table, first, parts, pieces):
        def body(t):
            at = {"x": t // 8, "y": lax.rem(t, 4)}
            core = lax.rem(t // 4, 2)
            blocks = []
            for z in range(4):
                at["z"] = z
                found = [p[(core,) + tuple(at[d] for d in order)] for p, (_, _, _, order) in zip(parts, pieces)]
                blocks.append(jnp.concatenate([f.astype(F32) for f in found], 1))
            table[pl.ds(pl.multiple_of(first + t * 32, 32), 32)] = jnp.concatenate(blocks, 0).astype(BF16)

        loop(32, body)

    assemble(hub_table, 0, hub_parts, HUB_PIECES)
    loads[0].wait()

    def before(i):
        cols = rows(i, 256)
        pre_self[:, cols] = dot(features[...], w_self[:, cols]) + bias[:, cols]
        total[:, cols] = dot(counts[:, :LOCAL], features[:, cols]) + dot(
            counts[:, LOCAL + SLOTS :], hub_table[:, cols]
        )

    loop(4, before)
    loads[2].wait()
    forward.wait_recv()

    def with_slots(i):
        cols = rows(i, 256)
        total[:, cols] += dot(counts[:, LOCAL : LOCAL + SLOTS], arrived[:, cols])

    loop(4, with_slots)

    def mean(i):
        scale = jnp.concatenate([inv_deg[rows(i, 64)]] * (WIDTH // 128), 1)
        aggregate[rows(i, 64)] = (total[rows(i, 64)] * scale).astype(BF16)

    loop(LOCAL // 64, mean)

    def act(i):
        m = rows(i, 128)
        pre = pre_self[m] + dot(aggregate[m], w_neigh[...])
        sigmoid = jax.nn.sigmoid(pre)
        hidden[m] = (pre * sigmoid).astype(BF16)
        slope = sigmoid * (1.0 + pre * (1.0 - sigmoid))
        d_pre[m] = (cotangent[m].astype(F32) * slope).astype(BF16)

    loop(LOCAL // 128, act)
    put_hidden = pltpu.make_async_copy(hidden, hidden_hbm, out_sem.at[0])
    put_hidden.start()

    def d_mean(i):
        cols = rows(i, 256)
        scale = jnp.concatenate([inv_deg[...]] * 2, 1)
        d_agg[:, cols] = (dot(d_pre[...], w_neigh_t[:, cols]) * scale).astype(BF16)

    loop(WIDTH // 256, d_mean)
    forward.wait_send()

    def d_slots(i):
        m = rows(i, 512)
        outgoing[m] = dot(counts_t[pl.ds(pl.multiple_of(LOCAL + i * 512, 512), 512)], d_agg[...]).astype(BF16)

    loop(SLOTS // 512, d_slots)
    backward.send(28)

    def keep_own(source, x, block):
        for core in range(2):
            if source == 0:
                own[0][core, x] = block[core].astype(BF16)
            elif source == 1:
                own[1][core, :, :, x] = block[core].astype(BF16)
            else:
                for y in range(4):
                    own[2][core, :, x, y] = block[core, y].astype(BF16)

    def grads_to(source, left):
        def body(i):
            block = dot(left[:, rows(i, 256)], d_pre[...], 0, 0).reshape(2, 4, 4, HUB, WIDTH)
            keep_own(source, i, block)

        loop(4, body)

    def d_hubs(i):
        base = LOCAL + SLOTS + i * 256
        block = dot(counts_t[pl.ds(pl.multiple_of(base, 256), 256)], d_agg[...])
        keep_own(2, i, block.reshape(2, 4, 4, HUB, WIDTH))

    def final_block(source, value):
        if source == 2:
            hub_back[...] = value
            return
        for part, (its_source, start, size, order) in zip(all_parts, GRAD_PIECES):
            if its_source == source:
                spot = (place["core"],) + tuple(place[d] for d in order)
                part[spot] = value[:, start : start + size].astype(BF16)

    reduce = Reduce(place, own, got, held, half, near, came, final_block, red_send, red_recv)
    spread = Spread(place, all_parts, [p[3] for p in GRAD_PIECES], [came[0]] * 4, all_send, all_recv)
    grads_to(0, features)
    first = reduce.start_core(0)
    grads_to(1, aggregate)
    second = reduce.start_core(1)
    backward.send(10)
    loop(4, d_hubs)
    third = reduce.start_core(2)
    reduce.finish_core(0, first)
    reduce.finish_core(1, second)
    reduce.finish_core(2, third)
    reduce.start_halves()
    backward.send(16)

    def own_grad(i):
        cols = rows(i, 256)
        total[:, cols] = dot(d_pre[...], w_self[cols], 1, 1) + dot(counts_t[:LOCAL], d_agg[:, cols])

    loop(4, own_grad)
    reduce.finish_halves()
    reduce.start_near()
    backward.send(20)
    reduce.finish_near()
    reduce.start_plane()
    backward.send(20)
    reduce.finish_plane()
    spread.start_plane()
    backward.send(18)
    spread.finish_plane()
    spread.start_last()
    backward.send(10)
    spread.relay()
    backward.send()
    backward.wait_recv()

    def final(i):
        cols = rows(i, 256)
        value = total[:, cols] + dot(picks_t[...], returned[:, cols])
        high = hub_back[:, cols].astype(BF16)
        low = (hub_back[:, cols] - high.astype(F32)).astype(BF16)
        both = jnp.concatenate([high.astype(F32), low.astype(F32)], 0).astype(BF16)
        grad_x[:, cols] = (value + dot(hub_picks[...], both, 0, 0)).astype(BF16)

    loop(4, final)
    put_grad_x = pltpu.make_async_copy(grad_x, grad_x_hbm, out_sem.at[1])
    put_grad_x.start()
    spread.finish_last()
    spread.finish_cores()
    puts = []
    for source, natural in enumerate((all_self, all_neigh)):
        pieces = [p for p in GRAD_PIECES if p[0] == source]
        parts = [part for part, p in zip(all_parts, GRAD_PIECES) if p[0] == source]
        assemble(arrived, source * WIDTH, parts, pieces)
        for k in range(4):
            put = pltpu.make_async_copy(
                arrived.at[pl.ds(source * WIDTH + k * 256, 256)],
                natural.at[pl.ds(k * 256, 256)],
                out_sem.at[2 + source * 4 + k],
            )
            put.start()
            puts.append(put)
    backward.wait_send()
    put_hidden.wait()
    put_grad_x.wait()
    for put in puts:
        put.wait()


def hand_out(*refs):
    sources, refs = refs[:4], refs[4:]
    results, bufs, (in_sem, out_sem) = refs[:4], refs[4:8], refs[8:]
    pieces = []
    for i, (src, dst, buf) in enumerate(zip(sources, results, bufs)):
        size = 256
        for k in range(src.shape[0] // size):
            part = pl.ds(k * size, size)
            slot = len(pieces)
            pieces.append(
                (
                    pltpu.make_async_copy(src.at[part], buf.at[part], in_sem.at[slot]),
                    pltpu.make_async_copy(buf.at[part], dst.at[part], out_sem.at[slot]),
                )
            )
    for load, _ in pieces:
        load.start()
    for load, store in pieces:
        load.wait()
        store.start()
    for _, store in pieces:
        store.wait()


def on_device(
    features, neighbours, degrees, send_rows, send_count, hub_rows, w_self, w_neigh, bias_term, cotangent
):
    vmem = pl.BlockSpec(memory_space=pltpu.VMEM)
    hbm = pl.BlockSpec(memory_space=pl.ANY)
    wide = (WIDTH,)

    def buf(*shape, kind=BF16):
        return pltpu.VMEM(shape, kind)

    part_bufs = [buf(2, 4, 4, 4, HUB, p[2]) for p in HUB_PIECES + GRAD_PIECES]
    for lead in ((2, 4, 4, 4), (4, 4, 4), (4, 4, 4), (4, 4), (2, 2, 4), (2, 4, 4), (15,)):
        part_bufs += [buf(*lead, HUB, WIDTH)] * 3
    dma = pltpu.SemaphoreType.DMA
    hidden, grad_x, grad_self, grad_neigh = pl.pallas_call(
        sage_kernel,
        out_shape=(
            jax.ShapeDtypeStruct((LOCAL, WIDTH), BF16),
            jax.ShapeDtypeStruct((LOCAL, WIDTH), BF16),
            jax.ShapeDtypeStruct((WIDTH, WIDTH), BF16),
            jax.ShapeDtypeStruct((WIDTH, WIDTH), BF16),
        ),
        in_specs=[vmem] * 5 + [pl.BlockSpec(memory_space=pltpu.SMEM)] + [vmem] + [hbm] * 3,
        out_specs=[hbm] * 4,
        scratch_shapes=[
            buf(LOCAL, WIDTH),
            buf(LOCAL, WIDTH),
            buf(WIDTH, WIDTH),
            buf(WIDTH, WIDTH),
            buf(WIDTH, WIDTH),
            buf(LOCAL, WIDTH),
            buf(LOCAL, SLOTS),
            buf(SLOT, LOCAL),
            buf(SLOTS, WIDTH),
            buf(SLOTS, WIDTH),
            buf(SLOTS, WIDTH),
            buf(HUBS, WIDTH),
            buf(FANOUT, 8, LOCAL, kind=jnp.int32),
            buf(TABLE, LOCAL),
            buf(LOCAL, TABLE),
            buf(LOCAL, 128, kind=F32),
            buf(LOCAL, WIDTH, kind=F32),
            buf(LOCAL, WIDTH, kind=F32),
            buf(LOCAL, WIDTH),
            buf(LOCAL, WIDTH),
            buf(LOCAL, WIDTH),
            buf(HUB, WIDTH, kind=F32),
            *part_bufs,
            dma((3,)),
            dma((10,)),
            dma,
            dma,
            dma,
            dma,
            dma((30,)),
            dma((30,)),
            dma((18,)),
            dma((18,)),
            dma((40,)),
            dma((40,)),
        ],
        compiler_params=pltpu.CompilerParams(
            collective_id=0, has_side_effects=True, vmem_limit_bytes=67043328
        ),
        name="sage",
    )(
        features,
        neighbours.T,
        degrees[None, :],
        send_rows,
        send_count,
        hub_rows,
        bias_term[None, :],
        w_self,
        w_neigh,
        cotangent,
    )
    results = (hidden, grad_x, grad_self, grad_neigh)
    return pl.pallas_call(
        hand_out,
        out_shape=tuple(jax.ShapeDtypeStruct(r.shape, r.dtype) for r in results),
        in_specs=[hbm] * 4,
        out_specs=[hbm] * 4,
        scratch_shapes=[buf(*r.shape) for r in results] + [dma((12,)), dma((12,))],
        name="hand_out",
    )(*results)


def solution(mesh):
    split = P(("row", "col"), None)
    in_specs = (split, split, P(("row", "col")), split, split, P(("row", "col")), P(), P(), P(), split)
    out_specs = (split, split, P(), P())
    return jax.shard_map(on_device, mesh=mesh, in_specs=in_specs, out_specs=out_specs, check_vma=False)
```

time: 181 us -> 170 us (0.939)
  local copies, waits for them, and re-layouts: 7.73 us -> 0 us
  Pallas kernels: 171 us -> 168 us
    pallas_call x1, Pallas kernels: 171 us -> 163 us  [on_device(): pl.pallas_call(sage_kernel, out_shape=(jax.ShapeDtypeStruct((LOCAL, WIDTH...]
    pallas_call x0 -> x1, Pallas kernels: none -> 5.47 us  [on_device(): pl.pallas_call(hand_out, out_shape=tuple((jax.ShapeDtypeStruct(r.shape, r...]
    slice x1 -> x0, local copies, waits for them, and re-layouts: 5.16 us -> none  [on_device(): return (hidden, grad_x, grads[:WIDTH], grads[WIDTH:])]
    unnamed x6 -> x0, local copies, waits for them, and re-layouts: 2.57 us -> none
where the time goes in v3:
time: 170 us; the launch traced here: 169 us
  Pallas kernels  168 us (99%)
    pallas_call x1, Pallas kernels, on_device(): pl.pallas_call(sage_kernel, out_shape=(jax.ShapeDtypeStruct((LOCAL, WIDTH...  163 us
    pallas_call x1, Pallas kernels, on_device(): pl.pallas_call(hand_out, out_shape=tuple((jax.ShapeDtypeStruct(r.shape, r...  5.47 us

profile of v3, /device:TPU:0, one launch (start us, length us, event | category | flops | bytes accessed | tf_op | source)
XLA Modules:
  0.0 169.0 jit_solution(9111867329285393302)
XLA Ops:
  0.6 162.8 %sage.1 = (bf16[512,1024]{1,0:T(8,128)(2,1)}, bf16[512,1024]{1,0:T(8,128)(2,1)}, bf16[1024,1024]{1,0:T(8,128)(2,1)}, bf16[1024,1024]{1,0:T(8,128)(2,1)}) custom-call(bf16[512,1024]{1,0:T(8,128)(2,1)} %features.1, s32[16,512]{1,0:T(8,128)} %bitcast.3, s32[1,512]{1,0:T(1,128)} %bitcast.5, s32[1,2048]{1,0:T(1,128)} %send_rows.1, s32[1,128]{1,0:T(1,128)} %send_count.1, ...), custom_call_target="tpu_custom_call" | custom-call | tf_op jit(solution)/shard_map/sage/pallas_call | solution.py:657
  163.5 5.5 %hand_out.1 = (bf16[512,1024]{1,0:T(8,128)(2,1)}, bf16[512,1024]{1,0:T(8,128)(2,1)}, bf16[1024,1024]{1,0:T(8,128)(2,1)}, bf16[1024,1024]{1,0:T(8,128)(2,1)}) custom-call(bf16[512,1024]{1,0:T(8,128)(2,1)} %get-tuple-element.8.refs_0_, bf16[512,1024]{1,0:T(8,128)(2,1)} %get-tuple-element.9.refs_1_, bf16[1024,1024]{1,0:T(8,128)(2,1)} %get-tuple-element.10.refs_2_, ...), custom_call_target="tpu_custom_call" | custom-call | tf_op jit(solution)/shard_map/hand_out/pallas_call | solution.py:721

commit v4 on v3

--- a/solution.py
+++ b/solution.py
@@ -73,6 +73,11 @@
 
 
 ORDER = message_order()
+GROUP = 32
+
+
+def opposite(offset):
+    return ((4 - offset[0]) % 4, offset[1], (4 - offset[2]) % 4, (4 - offset[3]) % 4)
 
 
 class Peers:
@@ -132,22 +137,36 @@
 
 
 class Exchange:
-    def __init__(self, peers, me, src, dst, send_sem, recv_sem):
+    def __init__(self, peers, me, src, dst, send_sem, recv_sem, back):
         self.peers, self.me, self.src, self.dst = peers, me, src, dst
         self.send_sem, self.recv_sem = send_sem, recv_sem
+        self.back = back
         self.sent = 0
 
     def send(self, count=PEERS):
-        for offset in ORDER[self.sent : self.sent + count]:
+        for message in range(self.sent, min(self.sent + count, PEERS - 1)):
+            here = pl.ds(message * SLOT, SLOT)
+            if self.back:
+                offset = opposite(ORDER[message])
+                src, dst, recv_sem = self.src.at[here], self.dst.at[rows(self.me, SLOT)], self.recv_sem
+            else:
+                offset = ORDER[message]
+                src, dst = self.src.at[rows(self.peers.rank(offset), SLOT)], self.dst.at[here]
+                recv_sem = self.recv_sem.at[message // GROUP]
             pltpu.make_async_remote_copy(
-                src_ref=self.src.at[rows(self.peers.rank(offset), SLOT)],
-                dst_ref=self.dst.at[rows(self.me, SLOT)],
+                src_ref=src,
+                dst_ref=dst,
                 send_sem=self.send_sem,
-                recv_sem=self.recv_sem,
+                recv_sem=recv_sem,
                 device_id=self.peers.device(offset),
                 device_id_type=MESH,
             ).start()
-        self.sent += count
+        self.sent = min(self.sent + count, PEERS - 1)
+
+    def wait_group(self, group):
+        count = min(GROUP, PEERS - 1 - group * GROUP)
+        part = pl.ds(group * GROUP * SLOT, count * SLOT)
+        pltpu.make_async_copy(self.src.at[part], self.dst.at[part], self.recv_sem.at[group]).wait()
 
     def wait_recv(self):
         most = pl.ds(0, SLOTS - SLOT)
@@ -162,27 +181,26 @@
     def __init__(self, place, outs, orders, sizes, send_sem, recv_sem):
         self.place, self.outs, self.orders, self.sizes = place, outs, orders, sizes
         self.send_sem, self.recv_sem = send_sem, recv_sem
-        self.passed = []
 
     def send(self, piece, spot, kind, peer):
         block = self.outs[piece].at[(self.place["core"],) + spot]
-        slot = piece * 10 + kind
+        slot = piece * 6 + kind
         copy = remote(block, block, self.send_sem.at[slot], self.recv_sem.at[slot], peer)
         copy.start()
         return copy
 
-    def hand_over(self, piece, spot, kind):
-        self.passed.append(self.send(piece, spot, kind, shifted(self.place, "core", 1)))
+    def hand_over(self, piece, spot):
+        self.send(piece, spot, 4, shifted(self.place, "core", 1))
 
     def start_plane(self):
         for steps in PLANE:
             for piece, order in enumerate(self.orders):
                 spot = tuple(self.place[d] for d in order)
-                self.send(piece, spot, 9, in_plane(self.place, order, steps))
+                self.send(piece, spot, 5, in_plane(self.place, order, steps))
 
     def finish_plane(self):
         for piece, size in enumerate(self.sizes):
-            wait_for(size.at[:, :, : self.outs[piece].shape[-1]], piece * 10 + 9, self.send_sem, self.recv_sem)
+            wait_for(size.at[:, :, : self.outs[piece].shape[-1]], piece * 6 + 5, self.send_sem, self.recv_sem)
 
     def start_last(self):
         self.copies = []
@@ -192,7 +210,7 @@
             down = self.send(piece, spot, 1, shifted(self.place, order[0], 3))
             self.copies.append((up, down))
         for piece, order in enumerate(self.orders):
-            self.hand_over(piece, (self.place[order[0]],), 4)
+            self.hand_over(piece, (self.place[order[0]],))
 
     def relay(self):
         relayed = []
@@ -201,10 +219,10 @@
             below, above = lax.rem(at + 3, 4), lax.rem(at + 1, 4)
             up.wait()
             first = self.send(piece, (below, pl.ds(0, 2)), 2, shifted(self.place, order[0], 1))
-            self.hand_over(piece, (below,), 5)
+            self.hand_over(piece, (below,))
             down.wait()
             second = self.send(piece, (above, pl.ds(2, 2)), 3, shifted(self.place, order[0], 3))
-            self.hand_over(piece, (above,), 6)
+            self.hand_over(piece, (above,))
             relayed.append((first, second))
         self.copies = relayed
 
@@ -213,11 +231,11 @@
             far = lax.rem(self.place[order[0]] + 2, 4)
             for half, copy in enumerate(self.copies[piece]):
                 copy.wait()
-                self.hand_over(piece, (far, pl.ds(2 * half, 2)), 7 + half)
+                self.hand_over(piece, (far, pl.ds(2 * half, 2)))
 
     def finish_cores(self):
-        for copy in self.passed:
-            copy.wait()
+        for piece, out in enumerate(self.outs):
+            wait_for(out.at[0], piece * 6 + 4, self.send_sem, self.recv_sem)
 
 
 class Reduce:
@@ -225,6 +243,7 @@
         self.place, self.own, self.got, self.held = place, own, got, held
         self.half, self.near, self.came, self.final = half, near, came, final
         self.send_sem, self.recv_sem = send_sem, recv_sem
+        self.copies = []
 
     def send(self, src, dst, slot, peer):
         copy = remote(src, dst, self.send_sem.at[slot], self.recv_sem.at[slot], peer)
@@ -246,14 +265,13 @@
 
         loop(16, add)
 
-    def start_halves(self):
-        self.copies = []
-        for source, order in enumerate(SUM_ORDERS):
-            far = lax.rem(self.place[order[0]] + 2, 4)
-            for i, step in enumerate((1, 3)):
-                part = self.held[0][source].at[far, pl.ds(2 * i, 2)]
-                peer = shifted(self.place, order[0], step)
-                self.copies.append(self.send(part, self.half[source].at[i], 3 + source * 2 + i, peer))
+    def start_halves(self, source):
+        order = SUM_ORDERS[source]
+        far = lax.rem(self.place[order[0]] + 2, 4)
+        for i, step in enumerate((1, 3)):
+            part = self.held[0][source].at[far, pl.ds(2 * i, 2)]
+            peer = shifted(self.place, order[0], step)
+            self.copies.append(self.send(part, self.half[source].at[i], 3 + source * 2 + i, peer))
 
     def finish_halves(self):
         for source, order in enumerate(SUM_ORDERS):
@@ -330,6 +348,7 @@
     returned,
     hub_table,
     nbr_wide,
+    first_id,
     counts_t,
     counts,
     inv_deg,
@@ -399,11 +418,11 @@
     own_hubs = dot(hub_picks[...], features[...])[:HUB]
     for part, (_, start, size, order) in zip(hub_parts, HUB_PIECES):
         part[(place["core"],) + tuple(place[d] for d in order)] = own_hubs[:, start : start + size].astype(BF16)
-    arrived[rows(me, SLOT)] = jnp.zeros((SLOT, WIDTH), BF16)
+    arrived[SLOTS - SLOT :] = jnp.zeros((SLOT, WIDTH), BF16)
     returned[rows(me, SLOT)] = jnp.zeros((SLOT, WIDTH), BF16)
 
-    forward = Exchange(peers, me, outgoing, arrived, fwd_send, fwd_recv)
-    backward = Exchange(peers, me, outgoing, returned, bwd_send, bwd_recv)
+    forward = Exchange(peers, me, outgoing, arrived, fwd_send, fwd_recv, False)
+    backward = Exchange(peers, me, outgoing, returned, bwd_send, bwd_recv, True)
     hub_spread = Spread(place, hub_parts, [p[3] for p in HUB_PIECES], [came[0]] * 3, hub_send, hub_recv)
     pl.semaphore_wait(barrier, PEERS - 1)
 
@@ -417,7 +436,8 @@
         def strip(i):
             base = b * 128 + i * 32
             sums = [jnp.zeros((8, LOCAL), F32) for _ in range(4)]
-            ids = [lax.broadcasted_iota(jnp.int32, (8, LOCAL), 0) + (base + 8 * g) for g in range(4)]
+            starts = [first_id[b * 8 + i * 2 + g // 2] + 8 * (g % 2) for g in range(4)]
+            ids = [lax.broadcasted_iota(jnp.int32, (8, LOCAL), 0) + start for start in starts]
             for j in range(FANOUT):
                 named = nbr_wide[j]
                 for g in range(4):
@@ -432,6 +452,15 @@
 
     hub_spread.start_plane()
     forward.send(30)
+
+    def natural(e):
+        first_id[e] = e * SLOT
+
+    loop(LOCAL // SLOT, natural)
+    loop(HUBS // SLOT, lambda e: natural((LOCAL + SLOTS) // SLOT + e))
+    for message, offset in enumerate(ORDER):
+        first_id[LOCAL // SLOT + message] = LOCAL + peers.rank(opposite(offset)) * SLOT
+    first_id[LOCAL // SLOT + PEERS - 1] = -2 * SLOT
     count_blocks(0, 14)
     hub_spread.finish_plane()
     hub_spread.start_last()
@@ -475,13 +504,21 @@
 
     loop(4, before)
     loads[2].wait()
-    forward.wait_recv()
-
-    def with_slots(i):
-        cols = rows(i, 256)
-        total[:, cols] += dot(counts[:, LOCAL : LOCAL + SLOTS], arrived[:, cols])
-
-    loop(4, with_slots)
+
+    def with_slots(group):
+        span = group * GROUP * SLOT
+        forward.wait_group(group)
+
+        def body(i):
+            cols = rows(i, 256)
+            total[:, cols] += dot(
+                counts[:, LOCAL + span : LOCAL + span + GROUP * SLOT], arrived[span : span + GROUP * SLOT, cols]
+            )
+
+        loop(4, body)
+
+    for group in range(4):
+        with_slots(group)
 
     def mean(i):
         scale = jnp.concatenate([inv_deg[rows(i, 64)]] * (WIDTH // 128), 1)
@@ -509,12 +546,10 @@
     loop(WIDTH // 256, d_mean)
     forward.wait_send()
 
-    def d_slots(i):
-        m = rows(i, 512)
-        outgoing[m] = dot(counts_t[pl.ds(pl.multiple_of(LOCAL + i * 512, 512), 512)], d_agg[...]).astype(BF16)
-
-    loop(SLOTS // 512, d_slots)
-    backward.send(28)
+    for i, messages in enumerate((8, 8, 8, 4)):
+        block = dot(counts_t[LOCAL + i * 512 : LOCAL + (i + 1) * 512], d_agg[...])
+        outgoing[i * 512 : (i + 1) * 512] = block.astype(BF16)
+        backward.send(messages)
 
     def keep_own(source, x, block):
         for core in range(2):
@@ -553,14 +588,16 @@
     first = reduce.start_core(0)
     grads_to(1, aggregate)
     second = reduce.start_core(1)
-    backward.send(10)
+    backward.send(8)
+    reduce.finish_core(0, first)
+    reduce.start_halves(0)
     loop(4, d_hubs)
     third = reduce.start_core(2)
-    reduce.finish_core(0, first)
     reduce.finish_core(1, second)
+    reduce.start_halves(1)
     reduce.finish_core(2, third)
-    reduce.start_halves()
-    backward.send(16)
+    reduce.start_halves(2)
+    backward.send(12)
 
     def own_grad(i):
         cols = rows(i, 256)
@@ -569,16 +606,16 @@
     loop(4, own_grad)
     reduce.finish_halves()
     reduce.start_near()
-    backward.send(20)
+    backward.send(14)
     reduce.finish_near()
     reduce.start_plane()
-    backward.send(20)
+    backward.send(14)
     reduce.finish_plane()
     spread.start_plane()
     backward.send(18)
     spread.finish_plane()
     spread.start_last()
-    backward.send(10)
+    backward.send(18)
     spread.relay()
     backward.send()
     backward.wait_recv()
@@ -678,6 +715,7 @@
             buf(SLOTS, WIDTH),
             buf(HUBS, WIDTH),
             buf(FANOUT, 8, LOCAL, kind=jnp.int32),
+            pltpu.SMEM((TABLE // SLOT,), jnp.int32),
             buf(TABLE, LOCAL),
             buf(LOCAL, TABLE),
             buf(LOCAL, 128, kind=F32),
@@ -691,15 +729,15 @@
             dma((3,)),
             dma((10,)),
             dma,
+            dma((4,)),
             dma,
             dma,
-            dma,
-            dma((30,)),
-            dma((30,)),
             dma((18,)),
             dma((18,)),
-            dma((40,)),
-            dma((40,)),
+            dma((18,)),
+            dma((18,)),
+            dma((24,)),
+            dma((24,)),
         ],
         compiler_params=pltpu.CompilerParams(
             collective_id=0, has_side_effects=True, vmem_limit_bytes=67043328

time: 170 us -> 169 us (level)
  no operation moved by 1% of the time
where the time goes in v4:
time: 169 us; the launch traced here: 168 us
  Pallas kernels  167 us (99%)
    pallas_call x1, Pallas kernels, on_device(): pl.pallas_call(sage_kernel, out_shape=(jax.ShapeDtypeStruct((LOCAL, WIDTH...  162 us
    pallas_call x1, Pallas kernels, on_device(): pl.pallas_call(hand_out, out_shape=tuple((jax.ShapeDtypeStruct(r.shape, r...  5.47 us

profile of v4, /device:TPU:0, one launch (start us, length us, event | category | flops | bytes accessed | tf_op | source)
XLA Modules:
  0.0 167.7 jit_solution(2481429602186124922)
XLA Ops:
  0.6 161.6 %sage.1 = (bf16[512,1024]{1,0:T(8,128)(2,1)}, bf16[512,1024]{1,0:T(8,128)(2,1)}, bf16[1024,1024]{1,0:T(8,128)(2,1)}, bf16[1024,1024]{1,0:T(8,128)(2,1)}) custom-call(bf16[512,1024]{1,0:T(8,128)(2,1)} %features.1, s32[16,512]{1,0:T(8,128)} %bitcast.3, s32[1,512]{1,0:T(1,128)} %bitcast.5, s32[1,2048]{1,0:T(1,128)} %send_rows.1, s32[1,128]{1,0:T(1,128)} %send_count.1, ...), custom_call_target="tpu_custom_call" | custom-call | tf_op jit(solution)/shard_map/sage/pallas_call | solution.py:694
  162.3 5.5 %hand_out.1 = (bf16[512,1024]{1,0:T(8,128)(2,1)}, bf16[512,1024]{1,0:T(8,128)(2,1)}, bf16[1024,1024]{1,0:T(8,128)(2,1)}, bf16[1024,1024]{1,0:T(8,128)(2,1)}) custom-call(bf16[512,1024]{1,0:T(8,128)(2,1)} %get-tuple-element.8.refs_0_, bf16[512,1024]{1,0:T(8,128)(2,1)} %get-tuple-element.9.refs_1_, bf16[1024,1024]{1,0:T(8,128)(2,1)} %get-tuple-element.10.refs_2_, ...), custom_call_target="tpu_custom_call" | custom-call | tf_op jit(solution)/shard_map/hand_out/pallas_call | solution.py:759

commit v5 on v4

--- a/solution.py
+++ b/solution.py
@@ -615,7 +615,7 @@
     backward.send(18)
     spread.finish_plane()
     spread.start_last()
-    backward.send(18)
+    backward.send(22)
     spread.relay()
     backward.send()
     backward.wait_recv()

time: 169 us -> 170 us (level)
  no operation moved by 1% of the time
where the time goes in v5:
time: 170 us; the launch traced here: 168 us
  Pallas kernels  168 us (99%)
    pallas_call x1, Pallas kernels, on_device(): pl.pallas_call(sage_kernel, out_shape=(jax.ShapeDtypeStruct((LOCAL, WIDTH...  162 us
    pallas_call x1, Pallas kernels, on_device(): pl.pallas_call(hand_out, out_shape=tuple((jax.ShapeDtypeStruct(r.shape, r...  5.47 us

profile of v5, /device:TPU:0, one launch (start us, length us, event | category | flops | bytes accessed | tf_op | source)
XLA Modules:
  0.0 168.4 jit_solution(7594357976633513147)
XLA Ops:
  0.6 162.3 %sage.1 = (bf16[512,1024]{1,0:T(8,128)(2,1)}, bf16[512,1024]{1,0:T(8,128)(2,1)}, bf16[1024,1024]{1,0:T(8,128)(2,1)}, bf16[1024,1024]{1,0:T(8,128)(2,1)}) custom-call(bf16[512,1024]{1,0:T(8,128)(2,1)} %features.1, s32[16,512]{1,0:T(8,128)} %bitcast.3, s32[1,512]{1,0:T(1,128)} %bitcast.5, s32[1,2048]{1,0:T(1,128)} %send_rows.1, s32[1,128]{1,0:T(1,128)} %send_count.1, ...), custom_call_target="tpu_custom_call" | custom-call | tf_op jit(solution)/shard_map/sage/pallas_call | solution.py:694
  163.0 5.5 %hand_out.1 = (bf16[512,1024]{1,0:T(8,128)(2,1)}, bf16[512,1024]{1,0:T(8,128)(2,1)}, bf16[1024,1024]{1,0:T(8,128)(2,1)}, bf16[1024,1024]{1,0:T(8,128)(2,1)}) custom-call(bf16[512,1024]{1,0:T(8,128)(2,1)} %get-tuple-element.8.refs_0_, bf16[512,1024]{1,0:T(8,128)(2,1)} %get-tuple-element.9.refs_1_, bf16[1024,1024]{1,0:T(8,128)(2,1)} %get-tuple-element.10.refs_2_, ...), custom_call_target="tpu_custom_call" | custom-call | tf_op jit(solution)/shard_map/hand_out/pallas_call | solution.py:759
